TPU v7x, 128 devices: a whole 4x4x4 slice. The times are simulated.
128 devices in a mesh: seq: 16 (over x_hi, y, core), tp: 8 (over x_lo, z).
Axes of the slice: x: 4 (x_hi: 2, x_lo: 2; x = x_hi * 2 + x_lo), y: 4, z: 4, core: 2. Of those that a mesh axis runs over, the one named last changes fastest.
Arguments:
- tokens: bfloat16 [8192, 1024], P('seq'), may hold values from -6 to 6
- segment_ids: int32 [8192], P('seq'), may hold values from 0 to 63, never falling along the last dimension, each value on 1 to 4608 neighbouring positions
- prefix_cache: bfloat16 [16384, 8, 128], P('seq', 'tp'), may hold values from -320 to 320
- norm1_gain: float32 [1024], replicated, may hold values from 0.5 to 1.5
- w_qkv: bfloat16 [1024, 8, 256], P(None, 'tp'), may hold values from -0.875 to 0.875
- w_out: bfloat16 [8, 128, 1024], P('tp'), may hold values from -0.1875 to 0.1875
- norm2_gain: float32 [1024], replicated, may hold values from 0.5 to 1.5
- expert_in: bfloat16 [32, 1024, 1024], P('seq'), may hold values from -0.1875 to 0.1875
- expert_out: bfloat16 [32, 512, 1024], P('seq'), may hold values from -0.25 to 0.25
- routes: int32 [8192, 8], P(('seq', 'tp')), may hold values from 0 to 31, all different within a row; in each aligned block of 64 rows (0 to 63, 64 to 127, ...) at most 32 rows name the same one
- route_weights: float32 [8192, 8], P(('seq', 'tp')), may hold values from 0.05 to 0.25
Outputs:
- hidden_out: bfloat16 [8192, 1024], P(('seq', 'tp'))
- new_cache: bfloat16 [8192, 8, 128], P('seq', 'tp')
Inputs may be any that keep to these rules, and one draw needn't show every extreme that they name: `segment_ids`: 64 requests lie in order of their numbers, each on 1 to 4608 consecutive new tokens, one on exactly that many. `routes`: each row names 8 different experts; in the rows of one device (aligned blocks of 64 rows) no expert is named by more than 32 rows, a bound that some block reaches.
All inputs are finite; a program needn't handle non-finite values.
Results may differ from a plain program's by a relative error of at most 0.02.
The roundings to bfloat16 on the way count: a program that leaves them out, or rounds other values in their place, can miss the bound.
Values may be sent and summed in bfloat16 or wider, within the bound.
No kernel may reach another device: no remote copies, remote signals or barrier semaphores. Data moves between devices by JAX's collectives and lax.ppermute only.
A program may use at most 128 MiB of HBM per device.

v0:
```python
import functools

import jax
import jax.numpy as jnp
from jax import lax
from jax.experimental import pallas as pl
from jax.experimental.pallas import tpu as pltpu
from jax.sharding import PartitionSpec as P

SCALE = 0.015625
EPS = 1e-06
HD = 64
NV = 80
TD = 512
PRE = 1024
ROWS = 64
TQ = 512
NQ = 2 * TD
SEG_AT = TD
PAY = SEG_AT + 16
MSG = 72
LIMIT = 1e26
NEG = -1e30
NT = (((1,), (1,)), ((), ()))
F32 = jnp.float32
BF = jnp.bfloat16


def seq_perm(move):
    return [
        (x * 8 + y * 2 + c, (lambda t: t[0] * 8 + t[1] * 2 + t[2])(move(x, y, c)))
        for x in range(2)
        for y in range(4)
        for c in range(2)
    ]


def tp_perm(move):
    return [(q * 4 + z, (lambda t: t[0] * 4 + t[1])(move(q, z))) for q in range(2) for z in range(4)]


CORE = seq_perm(lambda x, y, c: (x, y, 1 - c))
ACROSS = seq_perm(lambda x, y, c: (1 - x, y, c))
TURNS = (1, 3, 2)
SIDES = [
    (s * 8 + q * 4 + z, s * 8 + q * 4 + (z + (1 if s % 2 == 0 else 3)) % 4)
    for s in range(16)
    for q in range(2)
    for z in range(4)
]
CHIP_GROUPS = [[x * 8 + y * 2 + c for x in range(2) for y in range(4)] for c in range(2)]


def room(mib):
    return pltpu.CompilerParams(vmem_limit_bytes=mib << 20)


def rms(wide, gain):
    mean_square = jnp.mean(wide * wide, axis=-1, keepdims=True)
    return wide * lax.rsqrt(mean_square + EPS) * gain


def project_kernel(tok_ref, gain_ref, w_ref, seg_ref, pay_ref, ask_ref, row_ref, new_ref):
    normed = rms(tok_ref[...].astype(F32), gain_ref[...]).astype(BF)
    proj = jnp.dot(normed, w_ref[...], preferred_element_type=F32)
    ask_ref[:TD, :] = (proj[:, :128].astype(BF).astype(F32) * SCALE).astype(BF)
    new = proj[:, 128:].astype(BF)
    new_ref[...] = new
    pay_ref[:TD, :] = new
    seg = seg_ref[...].astype(F32)
    segs = jnp.concatenate([seg, jnp.full((12, 128), -1.0, F32)], axis=0).astype(BF)
    pay_ref[SEG_AT:, :] = segs
    ask_ref[SEG_AT:, :] = segs
    row = jnp.concatenate([seg[k : k + 1, :] for k in range(4)], axis=1)
    col = jnp.transpose(jnp.broadcast_to(row, (8, TD)))[:, 0:1]
    below = jnp.sum(jnp.where(col < row, 1.0, 0.0), axis=0, keepdims=True)
    row_ref[0:1, :] = jnp.concatenate([below, below], axis=1)
    row_ref[1:2, :] = jnp.concatenate([row, row], axis=1)


def values_t(kv):
    row = lax.broadcasted_iota(jnp.int32, (NV, 128), 0)
    col = lax.broadcasted_iota(jnp.int32, (NV, 128), 1)
    pick = jnp.where((col == row + HD) & (row < HD), 1.0, 0.0).astype(BF)
    vt = lax.dot_general(pick, kv, NT, preferred_element_type=F32)
    ones = lax.broadcasted_iota(jnp.int32, vt.shape, 0) >= HD
    return jnp.where(ones, 1.0, vt).astype(BF)


def online_step(q, kv, o_ref, m_ref, cols, mask):
    s = lax.dot_general(kv, q, NT, preferred_element_type=F32)
    if mask is not None:
        s = jnp.where(mask, s, NEG)
    m0 = m_ref[0:1, cols]
    m1 = jnp.maximum(m0, jnp.max(s, axis=0, keepdims=True))
    p = jnp.exp(s - m1).astype(BF)
    o_ref[:, cols] = o_ref[:, cols] * jnp.exp(m0 - m1) + jnp.dot(
        values_t(kv), p, preferred_element_type=F32
    )
    m_ref[0:1, cols] = m1


def spread_heads(stage, q_ref):
    wide = stage[...].astype(F32)
    low = lax.broadcasted_iota(jnp.int32, (TD, 128), 1) < HD
    q_ref[:TD, :] = jnp.where(low, wide, 0.0).astype(BF)
    q_ref[TD:, :] = jnp.where(low, pltpu.roll(wide, HD, 1), 0.0).astype(BF)


def fetch_all(pairs, sem):
    copies = [pltpu.make_async_copy(a, b, sem.at[i]) for i, (a, b) in enumerate(pairs)]
    for v in copies:
        v.start()
    return copies


def add_block(kv, q_ref, o_ref, m_ref, mask):
    vt = values_t(kv)
    for t in range(NQ // TQ):
        cols = pl.ds(t * TQ, TQ)
        s = lax.dot_general(kv, q_ref[cols, :], NT, preferred_element_type=F32)
        if mask is not None:
            s = jnp.where(mask(t * TQ, TQ), s, NEG)
        p = jnp.exp(s - m_ref[0:1, cols]).astype(BF)
        o_ref[:, cols] = o_ref[:, cols] + jnp.dot(vt, p, preferred_element_type=F32)


def too_large(o_ref):
    return jnp.logical_not(jnp.max(o_ref[HD : HD + 1, :]) < LIMIT)


def add_prefix(count, buf, sem, q_ref, o_ref, m_ref, head):
    def wait(j):
        pltpu.make_async_copy(buf.at[0], buf.at[j], sem.at[j]).wait()

    def block(j, _):
        if head:
            pl.when(j > 0)(lambda: wait(j))
        else:
            wait(j)
        add_block(buf[j], q_ref, o_ref, m_ref, None)
        return 0

    lax.fori_loop(0, count, block, 0, unroll=2)


def again_prefix(count, buf, q_ref, o_ref, m_ref):
    def again(i, _):
        kv = buf[i // 4, pl.ds(pl.multiple_of(i % 4 * 256, 256), 256), :]
        for t in range(NQ // 256):
            cols = pl.ds(t * 256, 256)
            online_step(q_ref[cols, :], kv, o_ref, m_ref, cols, None)
        return 0

    lax.fori_loop(0, count * 4, again, 0)


def masker(start, last, at, size):
    def mask(t, width):
        key = at + lax.broadcasted_iota(jnp.int32, (size, width), 0)
        ok = key >= start[:, t : t + width]
        return ok if last is None else ok & (key <= last[:, t : t + width])

    return mask


def add_suffix(low, whole, end, diagonal, start, last, buf, q_ref, o_ref, m_ref):
    def block(at, size, masked):
        at = pl.multiple_of(at, TD)
        bound = last if masked == "both" else None
        mask = masker(start, bound, at, size) if masked else None
        add_block(buf[pl.ds(at, size), :], q_ref, o_ref, m_ref, mask)

    ahead = end - whole
    split = lax.rem(ahead, 2)

    def partly(b, _):
        block(b * TD, TD, "start")
        return 0

    lax.fori_loop(low, whole, partly, 0)
    if diagonal:
        block(end * TD, TD, "both")
    pl.when(split == 1)(lambda: block(whole * TD, TD, None))

    def fully(b, _):
        block((whole + split + 2 * b) * TD, 2 * TD, None)
        return 0

    lax.fori_loop(0, ahead // 2, fully, 0)


def again_suffix(low, end, start, last, buf, q_ref, o_ref, m_ref):
    def again(i, _):
        at = pl.multiple_of(i * 256, 256)
        kv = buf[pl.ds(at, 256), :]
        mask = masker(start, last, at, 256)
        for t in range(4):
            online_step(
                q_ref[pl.ds(t * 256, 256), :], kv, o_ref, m_ref, pl.ds(t * 256, 256), mask(t * 256, 256)
            )
        return 0

    lax.fori_loop(low * 2, end * 2, again, 0)


def place():
    seq = lax.axis_index("seq")
    return seq // 8, lax.rem(seq // 2, 4), lax.rem(seq, 2)


def half_sources():
    x, y, c = place()
    rows = [y] + [lax.rem(y - k + 4, 4) for k in TURNS]
    return [r * 2 + d for r in rows for d in (c, 1 - c)]


def news_pairs(pays, buf, segs):
    src = half_sources()
    out = [(pays[j].at[pl.ds(SEG_AT, 16), :], segs.at[j]) for j in range(8)]
    for j in range(8):
        at = pl.multiple_of(src[j] * TD, TD)
        out.append((pays[j].at[pl.ds(0, TD), :], buf.at[pl.ds(at, TD), :]))
    return out


def count_same(segs, number, keep):
    total = jnp.zeros((16, 128), F32)
    for j in range(8):
        hit = segs[j].astype(F32) == jnp.where(keep[j], number, -2.0)
        total = total + jnp.where(hit, 1.0, 0.0)
    return jnp.sum(total).astype(jnp.int32)


def begin_kernel(ask_hbm, *refs, count):
    parts = refs[:count]
    o_ref, m_ref, stage, q_ref, buf, sem = refs[count:]
    copies = fetch_all(
        [(parts[j], buf.at[j]) for j in range(count)] + [(ask_hbm.at[pl.ds(0, TD), :], stage)], sem
    )
    o_ref[...] = jnp.zeros_like(o_ref)
    copies[count].wait()
    spread_heads(stage, q_ref)
    copies[0].wait()
    s = lax.dot_general(buf[0, :256, :], q_ref[...], NT, preferred_element_type=F32)
    m_ref[...] = jnp.broadcast_to(jnp.max(s, axis=0, keepdims=True), m_ref.shape)
    add_prefix(count, buf, sem, q_ref, o_ref, m_ref, True)

    @pl.when(too_large(o_ref))
    def _():
        o_ref[...] = jnp.zeros_like(o_ref)
        m_ref[...] = jnp.full_like(m_ref, NEG)
        again_prefix(count, buf, q_ref, o_ref, m_ref)


VM = pl.BlockSpec(memory_space=pltpu.VMEM)
HBM = pl.BlockSpec(memory_space=pl.ANY)
STATE = [jax.ShapeDtypeStruct((NV, NQ), F32), jax.ShapeDtypeStruct((8, NQ), F32)]
ASK = [pltpu.VMEM((TD, 128), BF), pltpu.VMEM((NQ, 128), BF)]


def price(keys):
    return pl.CostEstimate(
        flops=keys * NQ * 2 * 600, bytes_accessed=keys * 256, transcendentals=keys * NQ
    )


def begin_call(ask, parts):
    count = len(parts)
    return pl.pallas_call(
        functools.partial(begin_kernel, count=count),
        in_specs=[HBM] * (1 + count),
        out_specs=[VM, VM],
        out_shape=STATE,
        scratch_shapes=ASK
        + [pltpu.VMEM((count, PRE, 128), BF), pltpu.SemaphoreType.DMA((count + 1,))],
        cost_estimate=price(count * PRE),
        compiler_params=room(20),
        name="attend_prefix",
    )(ask, *parts)


def partner_kernel(ask_hbm, o_in, m_in, *refs):
    pays = refs[:8]
    out_ref, stage, marks, q_ref, o_ref, m_ref, buf, segs, sem = refs[8:]
    o_ref[...] = o_in[...]
    m_ref[...] = m_in[...]

    @pl.when(place()[0] == 0)
    def _():
        copies = fetch_all(
            news_pairs(pays, buf, segs)
            + [
                (ask_hbm.at[pl.ds(0, TD), :], stage),
                (ask_hbm.at[pl.ds(SEG_AT, 16), :], marks),
            ],
            sem,
        )
        for v in copies[:8] + copies[16:]:
            v.wait()
        spread_heads(stage, q_ref)
        newest = segs[0].astype(F32)
        for j in range(1, 8):
            newest = jnp.maximum(newest, segs[j].astype(F32))
        newest = jnp.max(newest)
        begin = 8 * TD - count_same(segs, newest, [True] * 8)
        seg = marks[...].astype(F32)
        row = jnp.concatenate([seg[k : k + 1, :] for k in range(4)], axis=1)
        row = jnp.concatenate([row, row], axis=1)
        start = jnp.where(row == newest, begin, 8 * TD)
        last = jnp.full((1, NQ), 8 * TD, jnp.int32)
        low = jnp.min(start) // TD
        whole = jnp.minimum((jnp.max(start) + TD - 1) // TD, 8)
        for v in copies[8:16]:
            v.wait()
        add_suffix(low, whole, 8, False, start, last, buf, q_ref, o_ref, m_ref)

        @pl.when(too_large(o_ref))
        def _():
            o_ref[...] = o_in[...]
            m_ref[...] = m_in[...]
            again_suffix(low, 8, start, last, buf, q_ref, o_ref, m_ref)

    out_ref[:HD, :] = o_ref[:HD, :]
    first = lax.broadcasted_iota(jnp.int32, (8, NQ), 0) == 0
    out_ref[HD:, :] = jnp.where(first, o_ref[HD : HD + 1, :], m_ref[0:1, :])


def partner_call(ask, state, pays):
    return pl.pallas_call(
        partner_kernel,
        in_specs=[HBM, VM, VM] + [HBM] * 8,
        out_specs=VM,
        out_shape=jax.ShapeDtypeStruct((MSG, NQ), F32),
        scratch_shapes=[
            ASK[0],
            pltpu.VMEM((16, 128), BF),
            ASK[1],
            pltpu.VMEM((NV, NQ), F32),
            pltpu.VMEM((8, NQ), F32),
            pltpu.VMEM((8 * TD, 128), BF),
            pltpu.VMEM((8, 16, 128), BF),
            pltpu.SemaphoreType.DMA((18,)),
        ],
        cost_estimate=price(3 * TD),
        compiler_params=room(20),
        name="attend_partner",
    )(ask, state[0], state[1], *pays)


def own_kernel(ask_hbm, row_ref, o_in, m_in, *refs):
    parts = refs[:6]
    pays = refs[6:14]
    out_ref, top_ref, stage, q_ref, o_ref, m_ref, pre, buf, segs, sem, pre_sem = refs[14:]
    x, y, c = place()
    asked = pltpu.make_async_copy(ask_hbm.at[pl.ds(0, TD), :], stage, sem.at[16])
    asked.start()
    fetch_all([(parts[j], pre.at[j]) for j in range(6)], pre_sem)
    copies = fetch_all(news_pairs(pays, buf, segs), sem)
    o_ref[...] = o_in[...]
    m_ref[...] = m_in[...]
    asked.wait()
    spread_heads(stage, q_ref)
    add_prefix(6, pre, pre_sem, q_ref, o_ref, m_ref, False)
    for v in copies:
        v.wait()
    own = y * 2 + c
    row = row_ref[1:2, :]
    mine = jnp.max(jnp.where(lax.broadcasted_iota(jnp.int32, (1, NQ), 1) == 0, row, -1.0))
    src = half_sources()
    begin = own * TD - count_same(segs, mine, [v < own for v in src])
    start = jnp.where(row == mine, begin, row_ref[0:1, :].astype(jnp.int32) + own * TD)
    lane = lax.broadcasted_iota(jnp.int32, (1, NQ), 1)
    last = own * TD + jnp.where(lane >= TD, lane - TD, lane)
    low = begin // TD
    whole = jnp.minimum((jnp.max(start) + TD - 1) // TD, own)
    add_suffix(low, whole, own, True, start, last, buf, q_ref, o_ref, m_ref)

    @pl.when(too_large(o_ref))
    def _():
        o_ref[...] = o_in[...]
        m_ref[...] = m_in[...]
        again_prefix(6, pre, q_ref, o_ref, m_ref)
        again_suffix(low, own + 1, start, last, buf, q_ref, o_ref, m_ref)

    out_ref[...] = o_ref[...]
    top_ref[...] = m_ref[...]


def own_call(ask, rows, state, parts, pays):
    return pl.pallas_call(
        own_kernel,
        in_specs=[HBM, VM, VM, VM] + [HBM] * 14,
        out_specs=[VM, VM],
        out_shape=STATE,
        scratch_shapes=ASK
        + [
            pltpu.VMEM((NV, NQ), F32),
            pltpu.VMEM((8, NQ), F32),
            pltpu.VMEM((6, PRE, 128), BF),
            pltpu.VMEM((8 * TD, 128), BF),
            pltpu.VMEM((8, 16, 128), BF),
            pltpu.SemaphoreType.DMA((17,)),
            pltpu.SemaphoreType.DMA((6,)),
        ],
        cost_estimate=price(9 * PRE),
        compiler_params=room(20),
        name="attend_own",
    )(ask, rows, state[0], state[1], *parts, *pays)


def join_kernel(o_ref, m_ref, msg_ref, out_ref):
    far = msg_ref[HD + 1 : HD + 2, :]
    near = m_ref[0:1, :]
    top = jnp.maximum(near, far)
    wa, wb = jnp.exp(near - top), jnp.exp(far - top)
    total = o_ref[: HD + 8, :] * wa + msg_ref[...] * wb
    mixed = total[:HD, :] / total[HD : HD + 1, :]
    both = jnp.concatenate([mixed[:, :TD], mixed[:, TD:]], axis=0)
    out_ref[...] = jnp.transpose(both).astype(BF)


def mix_kernel(
    att_ref, tok_hbm, gain_ref, route_ref, weight_ref, w0, w1, w2, w3, w4, res_ref, xi_ref, tok, sem
):
    tp = lax.axis_index("tp")
    fetch = pltpu.make_async_copy(
        tok_hbm.at[pl.ds(pl.multiple_of(tp * ROWS, ROWS), ROWS), :], tok, sem
    )
    fetch.start()
    q, z = tp // 4, lax.rem(tp, 4)
    side = 1 + 2 * place()[2]
    back = [0, side, 4 - side, 2]
    total = jnp.zeros((ROWS, 1024), F32)
    for j in range(4):
        row = lax.rem(z - back[j] + 4, 4)
        pair = jnp.concatenate([att_ref[q * 4 + row], att_ref[(1 - q) * 4 + row]], axis=1)
        w = jnp.concatenate([w0[0], w1[0]], axis=0) if j == 0 else (w2, w3, w4)[j - 1][...].reshape(256, 1024)
        total = total + jnp.dot(pair, w, preferred_element_type=F32)
    line = lax.broadcasted_iota(jnp.int32, (128, ROWS), 0)
    table = jnp.zeros((128, ROWS), F32)
    for k in range(8):
        expert = route_ref[k : k + 1, :]
        weight = weight_ref[k : k + 1, :]
        high = weight.astype(BF).astype(F32)
        table = table + jnp.where(line == expert, high, 0.0)
        table = table + jnp.where(line == expert + 32, weight - high, 0.0)
    gates = jnp.transpose(table).astype(BF)
    fetch.wait()
    total = tok[...].astype(F32) + total
    res_ref[...] = total
    xi = rms(total, gain_ref[...]).astype(BF)
    for j in range(8):
        xi_ref[j, :, :1024] = xi
        xi_ref[j, :, 1024:] = gates


def mix_call(att, tokens, gain, routes, weights, ws):
    return pl.pallas_call(
        mix_kernel,
        in_specs=[VM, HBM] + [VM] * 8,
        out_specs=[VM, VM],
        out_shape=[
            jax.ShapeDtypeStruct((ROWS, 1024), F32),
            jax.ShapeDtypeStruct((8, ROWS, 1152), BF),
        ],
        scratch_shapes=[pltpu.VMEM((ROWS, 1024), BF), pltpu.SemaphoreType.DMA],
        compiler_params=room(12),
        name="mix",
    )(att, tokens, gain, routes, weights, *ws)


def expert_kernel(x_ref, wi_own, wi_peer, wo_own, wo_peer, out_ref, acc):
    x, y, c = place()
    for e in range(4):
        wi, wo = ((wi_own, wo_own), (wi_peer, wo_peer))[e // 2]
        number = (x * 8 + y * 2 + (c if e < 2 else 1 - c)) * 2 + e % 2

        def half(h, _):
            rows = pl.ds(pl.multiple_of(h * 256, 256), 256)
            joined = jnp.dot(x_ref[rows, :1024], wi[e % 2], preferred_element_type=F32)
            g = joined[:, :512]
            hidden = (g / (1.0 + jnp.exp(-g)) * joined[:, 512:]).astype(BF)
            o = jnp.dot(hidden, wo[e % 2], preferred_element_type=F32).astype(BF).astype(F32)
            lane = lax.broadcasted_iota(jnp.int32, (256, 128), 1)
            hit = (lane == number) | (lane == number + 32)
            table = x_ref[rows, 1024:].astype(F32)
            gate = jnp.sum(jnp.where(hit, table, 0.0), axis=1, keepdims=True)
            o = o * gate
            if e:
                o = acc[rows, :] + o
            if e < 3:
                acc[rows, :] = o
            else:
                out_ref[rows, :] = o.astype(BF)
            return 0

        lax.fori_loop(0, 2, half, 0, unroll=2)


def expert_call(x, wi_own, wi_peer, wo_own, wo_peer):
    return pl.pallas_call(
        expert_kernel,
        in_specs=[VM] * 5,
        out_specs=VM,
        scratch_shapes=[pltpu.VMEM((512, 1024), F32)],
        out_shape=jax.ShapeDtypeStruct((512, 1024), BF),
        compiler_params=room(EXPERT_ROOM),
        name="experts",
    )(x, wi_own, wi_peer, wo_own, wo_peer)


EXPERT_ROOM = 30


def body(
    tokens,
    segment_ids,
    prefix_cache,
    norm1_gain,
    w_qkv,
    w_out,
    norm2_gain,
    expert_in,
    expert_out,
    routes,
    route_weights,
):
    tie = lax.optimization_barrier

    def swap(v):
        return lax.ppermute(v, "seq", CORE)

    def across(v):
        return lax.ppermute(v, "seq", ACROSS)

    def round_y(v):
        return [
            lax.ppermute(v, "seq", seq_perm(lambda a, b, d, k=k: (a, (b + k) % 4, d)))
            for k in TURNS
        ]

    pre = prefix_cache.reshape(PRE, 128)
    wx = lax.ppermute(w_out, "tp", tp_perm(lambda a, b: (1 - a, b)))
    far_pre = round_y(pre)
    near_pre = [swap(pre)]
    pay, ask, rows, new = pl.pallas_call(
        project_kernel,
        out_shape=[
            jax.ShapeDtypeStruct((PAY, 128), BF),
            jax.ShapeDtypeStruct((PAY, 128), BF),
            jax.ShapeDtypeStruct((8, NQ), F32),
            jax.ShapeDtypeStruct((TD, 128), BF),
        ],
        cost_estimate=pl.CostEstimate(flops=2 * TD * 1024 * 256, bytes_accessed=2 << 20, transcendentals=TD),
        compiler_params=room(12),
        name="project",
    )(tokens, norm1_gain[None, :], w_qkv.reshape(1024, 256), segment_ids.reshape(4, 128))
    asked = across(ask)
    first = begin_call(ask, [pre, near_pre[0]])

    far_pre, asked, first, pay = tie((far_pre, asked, first, pay))
    near_pre += [swap(v) for v in far_pre]
    near_new = [swap(pay)]
    near_new, pay = tie((near_new, pay))
    far_new = round_y(pay)
    wpair = jnp.concatenate([w_out, wx])
    side = lax.ppermute(wpair, ("seq", "tp"), SIDES)
    opposite = lax.ppermute(wpair, "tp", tp_perm(lambda a, b: (a, (b + 2) % 4)))
    shards = [v for p in zip([pre] + far_pre, near_pre) for v in p]
    second = begin_call(asked, shards)

    far_new, side, opposite, second = tie((far_new, side, opposite, second))
    near_new += [swap(v) for v in far_new]
    wz = [side, swap(side), opposite]
    pays = [v for p in zip([pay] + far_new, near_new) for v in p]
    message = partner_call(asked, second, pays)

    wz, near_new, message, expert_in_t, expert_out_t = tie(
        (wz, near_new, message, expert_in, expert_out)
    )
    returned = across(message)
    wi_peer = swap(expert_in_t)
    wo_peer = swap(expert_out_t)
    o, m = own_call(ask, rows, first, shards[2:], pays)
    attended = pl.pallas_call(
        join_kernel, out_shape=jax.ShapeDtypeStruct((TD, 128), BF), compiler_params=room(8), name="join"
    )(o, m, returned)

    spread = lax.all_to_all(attended.reshape(8, ROWS, 128), "tp", 0, 0, tiled=True)
    residual, copies = mix_call(
        spread,
        tokens,
        norm2_gain[None, :],
        jnp.transpose(routes),
        jnp.transpose(route_weights),
        [w_out, wx] + wz,
    )
    everyone = lax.all_to_all(copies, "seq", 0, 0, axis_index_groups=CHIP_GROUPS, tiled=True)
    partial = expert_call(
        everyone.reshape(512, 1152), expert_in, wi_peer, expert_out, wo_peer
    )
    back = lax.all_to_all(
        partial.reshape(8, ROWS, 1024), "seq", 0, 0, axis_index_groups=CHIP_GROUPS, tiled=True
    )
    hidden = (residual + jnp.sum(back.astype(F32), axis=0)).astype(BF)
    return hidden, new.reshape(TD, 1, 128)


def solution(mesh):
    in_specs = (
        P("seq", None),
        P("seq"),
        P("seq", "tp", None),
        P(),
        P(None, "tp", None),
        P("tp", None, None),
        P(),
        P("seq", None, None),
        P("seq", None, None),
        P(("seq", "tp"), None),
        P(("seq", "tp"), None),
    )
    out_specs = (P(("seq", "tp"), None), P("seq", "tp", None))
    return jax.shard_map(body, mesh=mesh, in_specs=in_specs, out_specs=out_specs, check_vma=False)
```

profile of v0, /device:TPU:0, one launch (start us, length us, event | category | flops | bytes accessed | tf_op | source)
XLA Modules:
  0.0 197.6 jit_solution(13766470685757119843)
XLA Ops:
  0.6 0.1 collective-permute-start.4
  0.7 3.4 %collective-permute-start.2 = (bf16[1024,128]{1,0:T(8,128)(2,1)}, bf16[1024,128]{1,0:T(8,128)(2,1)S(1)}, u32[]{:S(2)}, u32[]{:S(2)}) collective-permute-start(bf16[1024,128]{1,0:T(8,128)(2,1)} %bitcast.21), channel_id=1, source_target_pairs={{0,32},{8,40},{16,48},{24,56},{32,0},{40,8},{48,16},{56,24},{64,96... | collective-permute-start | bytes 786440 | tf_op jit(solution)/shard_map/ppermute | solution.py:539
  4.1 1.1 collective-permute-start.1
  5.1 1.0 collective-permute-start
  6.1 1.5 collective-permute-start.12
  7.6 1.2 copy-done.1
  8.8 1.0 copy-done.5
  9.9 0.7 copy-done.6
  10.6 0.7 copy-done.10
  11.2 1.3 project.1
  12.6 0.0 collective-permute-done.4.refs_1_
  12.6 2.7 %collective-permute-start.3 = (bf16[528,128]{1,0:T(8,128)(2,1)S(1)}, bf16[528,128]{1,0:T(8,128)(2,1)S(1)}, u32[]{:S(2)}, u32[]{:S(2)}) collective-permute-start(bf16[528,128]{1,0:T(8,128)(2,1)S(1)} %get-tuple-element.36.ask_hbm), channel_id=1, source_target_pairs={{0,64},{8,72},{16,80},{24,88},{32,96},{40,104},{48,112},{56,120},{... | collective-permute-start | bytes 405512 | tf_op jit(solution)/shard_map/ppermute | solution.py:535
  15.3 0.9 copy-done.11
  16.3 2.9 %attend_prefix.2 = (f32[80,1024]{1,0:T(8,128)S(1)}, f32[8,1024]{1,0:T(8,128)S(1)}) custom-call(bf16[528,128]{1,0:T(8,128)(2,1)S(1)} %get-tuple-element.36.ask_hbm, bf16[1024,128]{1,0:T(8,128)(2,1)S(1)} %bitcast.24, bf16[1024,128]{1,0:T(8,128)(2,1)S(1)} %collective-permute-done.4.refs_1_), custom_call_target="tpu_custom_call" | custom-call | flops 2516582400 | bytes 524288 | tf_op jit(solution)/shard_map/attend_prefix/pallas_call | solution.py:270
  19.2 0.1 collective-permute-done.3.ask_hbm
  19.2 0.0 collective-permute-done.2.refs_6_.refs_4_
  19.2 0.0 collective-permute-done.1.refs_4_.refs_2_
  19.2 0.1 collective-permute-start.5
  19.3 0.5 collective-permute-start.6
  19.8 0.1 collective-permute-start.7
  19.9 0.4 collective-permute-start.8
  20.4 10.6 %collective-permute-start.14 = (bf16[2,128,1024]{2,1,0:T(8,128)(2,1)S(1)}, bf16[2,128,1024]{2,1,0:T(8,128)(2,1)S(1)}, u32[]{:S(2)}, u32[]{:S(2)}) collective-permute-start(bf16[2,128,1024]{2,1,0:T(8,128)(2,1)S(1)} %constant_dynamic-update-slice_fusion), channel_id=1, source_target_pairs={{0,2},{1,3},{2,0},{3,1},{4,6},{5,7},{6,4},{7,5},{8,10},{9,11},{10,... | collective-permute-start | bytes 1572872 | tf_op jit(solution)/shard_map/ppermute | solution.py:569
  31.0 0.7 collective-permute-start.13
  31.8 0.7 collective-permute-start.11
  32.5 3.3 %collective-permute-start.10 = (bf16[528,128]{1,0:T(8,128)(2,1)S(1)}, bf16[528,128]{1,0:T(8,128)(2,1)S(1)}, u32[]{:S(2)}, u32[]{:S(2)}) collective-permute-start(bf16[528,128]{1,0:T(8,128)(2,1)S(1)} %get-tuple-element.47.refs_6_.refs_0_), channel_id=1, source_target_pairs={{0,48},{8,56},{16,0},{24,8},{32,16},{40,24},{48,32},{56,40},{64,11... | collective-permute-start | bytes 405512 | tf_op jit(solution)/shard_map/ppermute | solution.py:539
  35.8 0.9 collective-permute-start.9
  36.7 42.3 %attend_prefix.3 = (f32[80,1024]{1,0:T(8,128)S(1)}, f32[8,1024]{1,0:T(8,128)S(1)}) custom-call(bf16[528,128]{1,0:T(8,128)(2,1)S(1)} %collective-permute-done.3.ask_hbm, bf16[1024,128]{1,0:T(8,128)(2,1)S(1)} %bitcast.25, bf16[1024,128]{1,0:T(8,128)(2,1)S(1)} %collective-permute-done.4.refs_1_, bf16[1024,128]{1,0:T(8,128)(2,1)S(1)} %collective-permute-done.refs_2_.refs_0_, ...), custom_call_target="tpu_custom_call" | custom-call | flops 10066329600 | bytes 2097152 | tf_op jit(solution)/shard_map/attend_prefix/pallas_call | solution.py:270
  79.0 0.0 copy-start
  79.0 0.0 copy-start.3
  79.0 0.1 collective-permute-start.18
  79.1 0.5 collective-permute-start.15
  79.6 0.1 collective-permute-start.16
  79.7 0.4 collective-permute-start.17
  80.1 1.1 collective-permute-done.15.refs_9_.refs_3_
  81.2 0.2 collective-permute-done.16.refs_11_.refs_5_
  81.4 0.2 collective-permute-done.17.refs_13_.refs_7_
  81.6 7.0 %attend_partner.1 = f32[72,1024]{1,0:T(8,128)S(1)} custom-call(bf16[528,128]{1,0:T(8,128)(2,1)S(1)} %collective-permute-done.3.ask_hbm, f32[80,1024]{1,0:T(8,128)S(1)} %get-tuple-element.59.o_in, f32[8,1024]{1,0:T(8,128)S(1)} %get-tuple-element.60.m_in, bf16[528,128]{1,0:T(8,128)(2,1)S(1)} %get-tuple-element.47.refs_6_.refs_0_, ...), custom_call_target="tpu_custom_call" | custom-call | flops 1887436800 | bytes 393216 | tf_op jit(solution)/shard_map/attend_partner/pallas_call | solution.py:330
  88.6 0.2 collective-permute-start.20
  88.9 0.4 collective-permute-start.21
  89.2 37.1 %attend_own.1 = (f32[80,1024]{1,0:T(8,128)S(1)}, f32[8,1024]{1,0:T(8,128)S(1)}) custom-call(bf16[528,128]{1,0:T(8,128)(2,1)S(1)} %get-tuple-element.36.ask_hbm, f32[8,1024]{1,0:T(8,128)S(1)} %get-tuple-element.37.row_ref, f32[80,1024]{1,0:T(8,128)S(1)} %get-tuple-element.41.o_in, f32[8,1024]{1,0:T(8,128)S(1)} %get-tuple-element.42.m_in, ...), custom_call_target="tpu_custom_call" | custom-call | flops 11324620800 | bytes 2359296 | tf_op jit(solution)/shard_map/attend_own/pallas_call | solution.py:391
  126.3 0.1 join.1
  126.5 9.9 %all_to_all.15.att_ref = bf16[8,64,128]{2,1,0:T(8,128)(2,1)S(1)} all-to-all(bf16[8,64,128]{2,1,0:T(8,128)(2,1)S(1)} %bitcast.14), channel_id=1, replica_groups=mesh['seq'=16,'tp'=8] {'tp'}, dimensions={0} | all-to-all | bytes 262144 | tf_op jit(solution)/shard_map/all_to_all | solution.py:590
  136.4 0.9 mix.1
  137.3 30.6 %all_to_all.16 = bf16[8,64,1152]{2,1,0:T(8,128)(2,1)S(1)} all-to-all(bf16[8,64,1152]{2,1,0:T(8,128)(2,1)S(1)} %get-tuple-element.66), channel_id=1, replica_groups={{0,16,32,48,64,80,96,112},{8,24,40,56,72,88,104,120},{1,17,33,49,65,81,..., dimensions={0} | all-to-all | bytes 2359296 | tf_op jit(solution)/shard_map/all_to_all | solution.py:599
  167.9 7.4 %experts.1 = bf16[512,1024]{1,0:T(8,128)(2,1)S(1)} custom-call(bf16[512,1152]{1,0:T(8,128)(2,1)S(1)} %bitcast.11, bf16[2,1024,1024]{2,1,0:T(8,128)(2,1)S(1)} %copy-done, bf16[2,1024,1024]{2,1,0:T(8,128)(2,1)S(1)} %collective-permute-done.20.wi_peer, bf16[2,512,1024]{2,1,0:T(8,128)(2,1)S(1)} %copy-done.3, ...), custom_call_target="tpu_custom_call" | custom-call | tf_op jit(solution)/shard_map/experts/pallas_call | solution.py:502
  175.3 21.5 %all_to_all.17 = bf16[8,64,1024]{2,1,0:T(8,128)(2,1)S(1)} all-to-all(bf16[8,64,1024]{2,1,0:T(8,128)(2,1)S(1)} %bitcast.12), channel_id=1, replica_groups={{0,16,32,48,64,80,96,112},{8,24,40,56,72,88,104,120},{1,17,33,49,65,81,..., dimensions={0} | all-to-all | bytes 2097152 | tf_op jit(solution)/shard_map/all_to_all | solution.py:603
  196.8 0.2 convert_reduce_fusion
  196.9 0.7 add_convert_fusion
  (37 shorter events, 0.1 us)
Async XLA Ops:
  0.6 12.0 %collective-permute-start.4 = (bf16[1024,128]{1,0:T(8,128)(2,1)}, bf16[1024,128]{1,0:T(8,128)(2,1)S(1)}, u32[]{:S(2)}, u32[]{:S(2)}) collective-permute-start(bf16[1024,128]{1,0:T(8,128)(2,1)} %bitcast.20), channel_id=1, source_target_pairs={{0,8},{8,0},{16,24},{24,16},{32,40},{40,32},{48,56},{56,48},{64,72... | collective-permute-start | bytes 786440 | tf_op jit(solution)/shard_map/ppermute | solution.py:532
  0.7 18.5 %collective-permute-start.2 = (bf16[1024,128]{1,0:T(8,128)(2,1)}, bf16[1024,128]{1,0:T(8,128)(2,1)S(1)}, u32[]{:S(2)}, u32[]{:S(2)}) collective-permute-start(bf16[1024,128]{1,0:T(8,128)(2,1)} %bitcast.21), channel_id=1, source_target_pairs={{0,32},{8,40},{16,48},{24,56},{32,0},{40,8},{48,16},{56,24},{64,96... | collective-permute-start | bytes 786440 | tf_op jit(solution)/shard_map/ppermute | solution.py:539
  4.1 15.1 %collective-permute-start.1 = (bf16[1024,128]{1,0:T(8,128)(2,1)}, bf16[1024,128]{1,0:T(8,128)(2,1)S(1)}, u32[]{:S(2)}, u32[]{:S(2)}) collective-permute-start(bf16[1024,128]{1,0:T(8,128)(2,1)} %bitcast.22), channel_id=1, source_target_pairs={{0,48},{8,56},{16,0},{24,8},{32,16},{40,24},{48,32},{56,40},{64,11... | collective-permute-start | bytes 786440 | tf_op jit(solution)/shard_map/ppermute | solution.py:539
  5.1 14.1 %collective-permute-start = (bf16[1024,128]{1,0:T(8,128)(2,1)}, bf16[1024,128]{1,0:T(8,128)(2,1)S(1)}, u32[]{:S(2)}, u32[]{:S(2)}) collective-permute-start(bf16[1024,128]{1,0:T(8,128)(2,1)} %bitcast.23), channel_id=1, source_target_pairs={{0,16},{8,24},{16,32},{24,40},{32,48},{40,56},{48,0},{56,8},{64,80... | collective-permute-start | bytes 786440 | tf_op jit(solution)/shard_map/ppermute | solution.py:539
  6.1 14.2 %collective-permute-start.12 = (bf16[1,128,1024]{2,1,0:T(8,128)(2,1)}, bf16[1,128,1024]{2,1,0:T(8,128)(2,1)S(1)}, u32[]{:S(2)}, u32[]{:S(2)}) collective-permute-start(bf16[1,128,1024]{2,1,0:T(8,128)(2,1)} %w0.1), channel_id=1, source_target_pairs={{0,4},{1,5},{2,6},{3,7},{4,0},{5,1},{6,2},{7,3},{8,12},{9,13},{10,... | collective-permute-start | bytes 786440 | tf_op jit(solution)/shard_map/ppermute | solution.py:544
  7.6 1.2 copy-start.1
  8.8 1.0 copy-start.5
  9.9 0.7 copy-start.6
  10.6 0.7 copy-start.10
  12.6 7.7 %copy-start.4 = (bf16[1,128,1024]{2,1,0:T(8,128)(2,1)S(1)}, bf16[1,128,1024]{2,1,0:T(8,128)(2,1)}, u32[]{:S(2)}) copy-start(bf16[1,128,1024]{2,1,0:T(8,128)(2,1)} %w0.1) | copy-start | bytes 786436
  12.6 6.6 %collective-permute-start.3 = (bf16[528,128]{1,0:T(8,128)(2,1)S(1)}, bf16[528,128]{1,0:T(8,128)(2,1)S(1)}, u32[]{:S(2)}, u32[]{:S(2)}) collective-permute-start(bf16[528,128]{1,0:T(8,128)(2,1)S(1)} %get-tuple-element.36.ask_hbm), channel_id=1, source_target_pairs={{0,64},{8,72},{16,80},{24,88},{32,96},{40,104},{48,112},{56,120},{... | collective-permute-start | bytes 405512 | tf_op jit(solution)/shard_map/ppermute | solution.py:535
  15.3 0.9 copy-start.11
  16.3 20.4 %copy-start.12 = (bf16[1024,1,128]{2,0,1:T(8,128)(2,1)S(1)}, bf16[1024,1,128]{2,0,1:T(8,128)(2,1)}, u32[]{:S(2)}) copy-start(bf16[1024,1,128]{2,0,1:T(8,128)(2,1)} %param.13) | copy-start | bytes 786436
  19.2 12.5 %collective-permute-start.5 = (bf16[1024,128]{1,0:T(8,128)(2,1)S(1)}, bf16[1024,128]{1,0:T(8,128)(2,1)S(1)}, u32[]{:S(2)}, u32[]{:S(2)}) collective-permute-start(bf16[1024,128]{1,0:T(8,128)(2,1)S(1)} %collective-permute-done.refs_2_.refs_0_), channel_id=1, source_target_pairs={{0,8},{8,0},{16,24},{24,16},{32,40},{40,32},{48,56},{56,48},{64,72... | collective-permute-start | bytes 786440 | tf_op jit(solution)/shard_map/ppermute | solution.py:532
  19.3 13.2 %collective-permute-start.6 = (bf16[1024,128]{1,0:T(8,128)(2,1)S(1)}, bf16[1024,128]{1,0:T(8,128)(2,1)S(1)}, u32[]{:S(2)}, u32[]{:S(2)}) collective-permute-start(bf16[1024,128]{1,0:T(8,128)(2,1)S(1)} %collective-permute-done.1.refs_4_.refs_2_), channel_id=1, source_target_pairs={{0,8},{8,0},{16,24},{24,16},{32,40},{40,32},{48,56},{56,48},{64,72... | collective-permute-start | bytes 786440 | tf_op jit(solution)/shard_map/ppermute | solution.py:532
  19.8 16.0 %collective-permute-start.7 = (bf16[1024,128]{1,0:T(8,128)(2,1)S(1)}, bf16[1024,128]{1,0:T(8,128)(2,1)S(1)}, u32[]{:S(2)}, u32[]{:S(2)}) collective-permute-start(bf16[1024,128]{1,0:T(8,128)(2,1)S(1)} %collective-permute-done.2.refs_6_.refs_4_), channel_id=1, source_target_pairs={{0,8},{8,0},{16,24},{24,16},{32,40},{40,32},{48,56},{56,48},{64,72... | collective-permute-start | bytes 786440 | tf_op jit(solution)/shard_map/ppermute | solution.py:532
  19.9 11.1 %collective-permute-start.8 = (bf16[528,128]{1,0:T(8,128)(2,1)S(1)}, bf16[528,128]{1,0:T(8,128)(2,1)S(1)}, u32[]{:S(2)}, u32[]{:S(2)}) collective-permute-start(bf16[528,128]{1,0:T(8,128)(2,1)S(1)} %get-tuple-element.47.refs_6_.refs_0_), channel_id=1, source_target_pairs={{0,8},{8,0},{16,24},{24,16},{32,40},{40,32},{48,56},{56,48},{64,72... | collective-permute-start | bytes 405512 | tf_op jit(solution)/shard_map/ppermute | solution.py:532
  20.4 58.6 %collective-permute-start.14 = (bf16[2,128,1024]{2,1,0:T(8,128)(2,1)S(1)}, bf16[2,128,1024]{2,1,0:T(8,128)(2,1)S(1)}, u32[]{:S(2)}, u32[]{:S(2)}) collective-permute-start(bf16[2,128,1024]{2,1,0:T(8,128)(2,1)S(1)} %constant_dynamic-update-slice_fusion), channel_id=1, source_target_pairs={{0,2},{1,3},{2,0},{3,1},{4,6},{5,7},{6,4},{7,5},{8,10},{9,11},{10,... | collective-permute-start | bytes 1572872 | tf_op jit(solution)/shard_map/ppermute | solution.py:569
  31.0 47.9 %collective-permute-start.13 = (bf16[2,128,1024]{2,1,0:T(8,128)(2,1)S(1)}, bf16[2,128,1024]{2,1,0:T(8,128)(2,1)S(1)}, u32[]{:S(2)}, u32[]{:S(2)}) collective-permute-start(bf16[2,128,1024]{2,1,0:T(8,128)(2,1)S(1)} %constant_dynamic-update-slice_fusion), channel_id=1, source_target_pairs={{0,1},{1,2},{2,3},{3,0},{4,5},{5,6},{6,7},{7,4},{8,11},{9,8},{10,9... | collective-permute-start | bytes 1572872 | tf_op jit(solution)/shard_map/ppermute | solution.py:568
  31.8 47.2 %collective-permute-start.11 = (bf16[528,128]{1,0:T(8,128)(2,1)S(1)}, bf16[528,128]{1,0:T(8,128)(2,1)S(1)}, u32[]{:S(2)}, u32[]{:S(2)}) collective-permute-start(bf16[528,128]{1,0:T(8,128)(2,1)S(1)} %get-tuple-element.47.refs_6_.refs_0_), channel_id=1, source_target_pairs={{0,32},{8,40},{16,48},{24,56},{32,0},{40,8},{48,16},{56,24},{64,96... | collective-permute-start | bytes 405512 | tf_op jit(solution)/shard_map/ppermute | solution.py:539
  32.5 46.4 %collective-permute-start.10 = (bf16[528,128]{1,0:T(8,128)(2,1)S(1)}, bf16[528,128]{1,0:T(8,128)(2,1)S(1)}, u32[]{:S(2)}, u32[]{:S(2)}) collective-permute-start(bf16[528,128]{1,0:T(8,128)(2,1)S(1)} %get-tuple-element.47.refs_6_.refs_0_), channel_id=1, source_target_pairs={{0,48},{8,56},{16,0},{24,8},{32,16},{40,24},{48,32},{56,40},{64,11... | collective-permute-start | bytes 405512 | tf_op jit(solution)/shard_map/ppermute | solution.py:539
  35.8 43.2 %collective-permute-start.9 = (bf16[528,128]{1,0:T(8,128)(2,1)S(1)}, bf16[528,128]{1,0:T(8,128)(2,1)S(1)}, u32[]{:S(2)}, u32[]{:S(2)}) collective-permute-start(bf16[528,128]{1,0:T(8,128)(2,1)S(1)} %get-tuple-element.47.refs_6_.refs_0_), channel_id=1, source_target_pairs={{0,16},{8,24},{16,32},{24,40},{32,48},{40,56},{48,0},{56,8},{64,80... | collective-permute-start | bytes 405512 | tf_op jit(solution)/shard_map/ppermute | solution.py:539
  79.0 9.6 %copy-start = (bf16[2,1024,1024]{2,1,0:T(8,128)(2,1)S(1)}, bf16[2,1024,1024]{2,1,0:T(8,128)(2,1)}, u32[]{:S(2)}) copy-start(bf16[2,1024,1024]{2,1,0:T(8,128)(2,1)} %wi_own.1) | copy-start | bytes 12582916
  79.0 9.9 %copy-start.3 = (bf16[2,512,1024]{2,1,0:T(8,128)(2,1)S(1)}, bf16[2,512,1024]{2,1,0:T(8,128)(2,1)}, u32[]{:S(2)}) copy-start(bf16[2,512,1024]{2,1,0:T(8,128)(2,1)} %wo_own.1) | copy-start | bytes 6291460
  79.0 9.6 %collective-permute-start.18 = (bf16[2,128,1024]{2,1,0:T(8,128)(2,1)S(1)}, bf16[2,128,1024]{2,1,0:T(8,128)(2,1)S(1)}, u32[]{:S(2)}, u32[]{:S(2)}) collective-permute-start(bf16[2,128,1024]{2,1,0:T(8,128)(2,1)S(1)} %collective-permute-done.13.w2), channel_id=1, source_target_pairs={{0,8},{8,0},{16,24},{24,16},{32,40},{40,32},{48,56},{56,48},{64,72... | collective-permute-start | bytes 1572872 | tf_op jit(solution)/shard_map/ppermute | solution.py:532
  79.1 2.1 %collective-permute-start.15 = (bf16[528,128]{1,0:T(8,128)(2,1)S(1)}, bf16[528,128]{1,0:T(8,128)(2,1)S(1)}, u32[]{:S(2)}, u32[]{:S(2)}) collective-permute-start(bf16[528,128]{1,0:T(8,128)(2,1)S(1)} %collective-permute-done.9.refs_8_.refs_2_), channel_id=1, source_target_pairs={{0,8},{8,0},{16,24},{24,16},{32,40},{40,32},{48,56},{56,48},{64,72... | collective-permute-start | bytes 405512 | tf_op jit(solution)/shard_map/ppermute | solution.py:532
  79.6 1.8 collective-permute-start.16
  79.7 1.9 collective-permute-start.17
  88.6 79.2 %collective-permute-start.20 = (bf16[2,1024,1024]{2,1,0:T(8,128)(2,1)S(1)}, bf16[2,1024,1024]{2,1,0:T(8,128)(2,1)S(1)}, u32[]{:S(2)}, u32[]{:S(2)}) collective-permute-start(bf16[2,1024,1024]{2,1,0:T(8,128)(2,1)S(1)} %copy-done), channel_id=1, source_target_pairs={{0,8},{8,0},{16,24},{24,16},{32,40},{40,32},{48,56},{56,48},{64,72... | collective-permute-start | bytes 12582920 | tf_op jit(solution)/shard_map/ppermute | solution.py:532
  88.9 37.5 %collective-permute-start.19 = (f32[72,1024]{1,0:T(8,128)S(1)}, f32[72,1024]{1,0:T(8,128)S(1)}, u32[]{:S(2)}, u32[]{:S(2)}) collective-permute-start(f32[72,1024]{1,0:T(8,128)S(1)} %attend_partner.1), channel_id=1, source_target_pairs={{0,64},{8,72},{16,80},{24,88},{32,96},{40,104},{48,112},{56,120},{... | collective-permute-start | bytes 884744 | tf_op jit(solution)/shard_map/ppermute | solution.py:535
  88.9 79.0 %collective-permute-start.21 = (bf16[2,512,1024]{2,1,0:T(8,128)(2,1)S(1)}, bf16[2,512,1024]{2,1,0:T(8,128)(2,1)S(1)}, u32[]{:S(2)}, u32[]{:S(2)}) collective-permute-start(bf16[2,512,1024]{2,1,0:T(8,128)(2,1)S(1)} %copy-done.3), channel_id=1, source_target_pairs={{0,8},{8,0},{16,24},{24,16},{32,40},{40,32},{48,56},{56,48},{64,72... | collective-permute-start | bytes 6291464 | tf_op jit(solution)/shard_map/ppermute | solution.py:532
  89.2 47.1 %copy-start.2 = (bf16[512,1024]{1,0:T(8,128)(2,1)S(1)}, bf16[512,1024]{1,0:T(8,128)(2,1)}, u32[]{:S(2)}) copy-start(bf16[512,1024]{1,0:T(8,128)(2,1)} %tok_hbm.1) | copy-start | bytes 3145732
  89.2 47.1 %copy-start.7 = (f32[1024]{0:T(1024)S(1)}, f32[1024]{0:T(1024)}, u32[]{:S(2)}) copy-start(f32[1024]{0:T(1024)} %param.17) | copy-start | bytes 12292
  89.2 47.1 %copy-start.8 = (s32[64,8]{0,1:T(8,128)S(1)}, s32[64,8]{0,1:T(8,128)}, u32[]{:S(2)}) copy-start(s32[64,8]{0,1:T(8,128)} %param.20) | copy-start | bytes 6148
  89.2 47.1 %copy-start.9 = (f32[64,8]{0,1:T(8,128)S(1)}, f32[64,8]{0,1:T(8,128)}, u32[]{:S(2)}) copy-start(f32[64,8]{0,1:T(8,128)} %param.21) | copy-start | bytes 6148
where the time goes:
time: 199 us; the launch traced here: 198 us
  Pallas kernels  99 us (50%)
  blocking collectives  62 us (31%)
  starting transfers between devices  28.7 us (14%)
  local copies, waits for them, and re-layouts  4.65 us (2%)
    pallas_call x2, Pallas kernels, begin_call(): pl.pallas_call(functools.partial(begin_kernel, count=count), in_specs=[HB...  45.1 us
    pallas_call x1, Pallas kernels, own_call(): pl.pallas_call(own_kernel, in_specs=[HBM, VM, VM, VM] + [HBM] * 14, out_s...  37.1 us
    all_to_all x1, blocking collectives, body(): lax.all_to_all(copies, 'seq', 0, 0, axis_index_groups=CHIP_GROUPS, tiled=...  30.6 us
    all_to_all x1, blocking collectives, body(): lax.all_to_all(partial.reshape(8, ROWS, 1024), 'seq', 0, 0, axis_index_gr...  21.5 us
    ppermute x1, starting transfers between devices, body(): opposite = lax.ppermute(wpair, 'tp', tp_perm(lambda a, b: (a, (b + 2) % 4)))  10.6 us
    ppermute x6, starting transfers between devices, round_y(): lax.ppermute(v, 'seq', seq_perm(lambda a, b, d, k=k: (a, (b + k) % 4, d)))  10.2 us
    all_to_all x1, blocking collectives, body(): lax.all_to_all(attended.reshape(8, ROWS, 128), 'tp', 0, 0, tiled=True)  9.89 us
    pallas_call x1, Pallas kernels, expert_call(): pl.pallas_call(expert_kernel, in_specs=[VM] * 5, out_specs=VM, scratch_sh...  7.43 us
  transfers between devices with their start and end apart: 22, of which 4 were waited for; matrix products, arithmetic and copies ran while one was open for 0% of the time, Pallas kernels for 46%

commit v1 on v0

--- a/solution.py
+++ b/solution.py
@@ -60,14 +60,23 @@
     return wide * lax.rsqrt(mean_square + EPS) * gain
 
 
-def project_kernel(tok_ref, gain_ref, w_ref, seg_ref, pay_ref, ask_ref, row_ref, new_ref):
-    normed = rms(tok_ref[...].astype(F32), gain_ref[...]).astype(BF)
-    proj = jnp.dot(normed, w_ref[...], preferred_element_type=F32)
-    ask_ref[:TD, :] = (proj[:, :128].astype(BF).astype(F32) * SCALE).astype(BF)
-    new = proj[:, 128:].astype(BF)
-    new_ref[...] = new
-    pay_ref[:TD, :] = new
-    seg = seg_ref[...].astype(F32)
+def project_kernel(
+    tok_hbm, gain_hbm, w_hbm, seg_hbm, pay_ref, ask_ref, row_ref, new_ref, tok, gain, w, seg_in, sem
+):
+    small = [
+        pltpu.make_async_copy(w_hbm, w, sem.at[4]),
+        pltpu.make_async_copy(gain_hbm, gain, sem.at[5]),
+        pltpu.make_async_copy(seg_hbm, seg_in, sem.at[6]),
+    ]
+    large = [
+        pltpu.make_async_copy(tok_hbm.at[pl.ds(i * 128, 128), :], tok.at[pl.ds(i * 128, 128), :], sem.at[i])
+        for i in range(4)
+    ]
+    for v in [large[0]] + small + large[1:]:
+        v.start()
+    for v in small:
+        v.wait()
+    seg = seg_in[...].astype(F32)
     segs = jnp.concatenate([seg, jnp.full((12, 128), -1.0, F32)], axis=0).astype(BF)
     pay_ref[SEG_AT:, :] = segs
     ask_ref[SEG_AT:, :] = segs
@@ -76,6 +85,16 @@
     below = jnp.sum(jnp.where(col < row, 1.0, 0.0), axis=0, keepdims=True)
     row_ref[0:1, :] = jnp.concatenate([below, below], axis=1)
     row_ref[1:2, :] = jnp.concatenate([row, row], axis=1)
+    for i in range(2):
+        large[2 * i].wait()
+        large[2 * i + 1].wait()
+        rows = pl.ds(i * 256, 256)
+        normed = rms(tok[rows, :].astype(F32), gain[...]).astype(BF)
+        proj = jnp.dot(normed, w[...], preferred_element_type=F32)
+        ask_ref[rows, :] = (proj[:, :128].astype(BF).astype(F32) * SCALE).astype(BF)
+        new = proj[:, 128:].astype(BF)
+        new_ref[rows, :] = new
+        pay_ref[rows, :] = new
 
 
 def values_t(kv):
@@ -114,14 +133,14 @@
     return copies
 
 
-def add_block(kv, q_ref, o_ref, m_ref, mask):
+def add_block(kv, q_ref, o_ref, m_ref, mask, level=0):
     vt = values_t(kv)
     for t in range(NQ // TQ):
         cols = pl.ds(t * TQ, TQ)
         s = lax.dot_general(kv, q_ref[cols, :], NT, preferred_element_type=F32)
         if mask is not None:
             s = jnp.where(mask(t * TQ, TQ), s, NEG)
-        p = jnp.exp(s - m_ref[0:1, cols]).astype(BF)
+        p = jnp.exp(s - m_ref[level : level + 1, cols]).astype(BF)
         o_ref[:, cols] = o_ref[:, cols] + jnp.dot(vt, p, preferred_element_type=F32)
 
 
@@ -164,30 +183,27 @@
     return mask
 
 
-def add_suffix(low, whole, end, diagonal, start, last, buf, q_ref, o_ref, m_ref):
-    def block(at, size, masked):
+def add_suffix(low, end, diagonal, start, last, reach, buf, q_ref, o_ref, m_ref):
+    m_ref[1:2, :] = jnp.where(reach, m_ref[0:1, :], -NEG)
+
+    def block(at, size, masked, level=0):
         at = pl.multiple_of(at, TD)
         bound = last if masked == "both" else None
         mask = masker(start, bound, at, size) if masked else None
-        add_block(buf[pl.ds(at, size), :], q_ref, o_ref, m_ref, mask)
-
-    ahead = end - whole
-    split = lax.rem(ahead, 2)
-
-    def partly(b, _):
-        block(b * TD, TD, "start")
-        return 0
-
-    lax.fori_loop(low, whole, partly, 0)
+        add_block(buf[pl.ds(at, size), :], q_ref, o_ref, m_ref, mask, level)
+
+    pl.when(low < end)(lambda: block(low * TD, TD, "start"))
     if diagonal:
         block(end * TD, TD, "both")
-    pl.when(split == 1)(lambda: block(whole * TD, TD, None))
+    between = jnp.maximum(end - 1 - low, 0)
+    split = lax.rem(between, 2)
+    pl.when(split == 1)(lambda: block((low + 1) * TD, TD, None, 1))
 
     def fully(b, _):
-        block((whole + split + 2 * b) * TD, 2 * TD, None)
+        block((low + 1 + split + 2 * b) * TD, 2 * TD, None, 1)
         return 0
 
-    lax.fori_loop(0, ahead // 2, fully, 0)
+    lax.fori_loop(0, between // 2, fully, 0)
 
 
 def again_suffix(low, end, start, last, buf, q_ref, o_ref, m_ref):
@@ -255,6 +271,7 @@
 
 VM = pl.BlockSpec(memory_space=pltpu.VMEM)
 HBM = pl.BlockSpec(memory_space=pl.ANY)
+FAR = pl.BlockSpec(memory_space=pltpu.HBM)
 STATE = [jax.ShapeDtypeStruct((NV, NQ), F32), jax.ShapeDtypeStruct((8, NQ), F32)]
 ASK = [pltpu.VMEM((TD, 128), BF), pltpu.VMEM((NQ, 128), BF)]
 
@@ -269,7 +286,7 @@
     count = len(parts)
     return pl.pallas_call(
         functools.partial(begin_kernel, count=count),
-        in_specs=[HBM] * (1 + count),
+        in_specs=[HBM, FAR] + [HBM] * (count - 1),
         out_specs=[VM, VM],
         out_shape=STATE,
         scratch_shapes=ASK
@@ -310,10 +327,9 @@
         start = jnp.where(row == newest, begin, 8 * TD)
         last = jnp.full((1, NQ), 8 * TD, jnp.int32)
         low = jnp.min(start) // TD
-        whole = jnp.minimum((jnp.max(start) + TD - 1) // TD, 8)
         for v in copies[8:16]:
             v.wait()
-        add_suffix(low, whole, 8, False, start, last, buf, q_ref, o_ref, m_ref)
+        add_suffix(low, 8, False, start, None, row == newest, buf, q_ref, o_ref, m_ref)
 
         @pl.when(too_large(o_ref))
         def _():
@@ -373,8 +389,7 @@
     lane = lax.broadcasted_iota(jnp.int32, (1, NQ), 1)
     last = own * TD + jnp.where(lane >= TD, lane - TD, lane)
     low = begin // TD
-    whole = jnp.minimum((jnp.max(start) + TD - 1) // TD, own)
-    add_suffix(low, whole, own, True, start, last, buf, q_ref, o_ref, m_ref)
+    add_suffix(low, own, True, start, last, row == mine, buf, q_ref, o_ref, m_ref)
 
     @pl.when(too_large(o_ref))
     def _():
@@ -552,8 +567,17 @@
             jax.ShapeDtypeStruct((8, NQ), F32),
             jax.ShapeDtypeStruct((TD, 128), BF),
         ],
-        cost_estimate=pl.CostEstimate(flops=2 * TD * 1024 * 256, bytes_accessed=2 << 20, transcendentals=TD),
-        compiler_params=room(12),
+        in_specs=[FAR] * 4,
+        scratch_shapes=[
+            pltpu.VMEM((TD, 1024), BF),
+            pltpu.VMEM((1, 1024), F32),
+            pltpu.VMEM((1024, 256), BF),
+            pltpu.VMEM((4, 128), jnp.int32),
+            pltpu.SemaphoreType.DMA((7,)),
+        ],
+        cost_estimate=pl.CostEstimate(
+            flops=2 * TD * 1024 * 256, bytes_accessed=2 << 20, transcendentals=TD
+        ),
         name="project",
     )(tokens, norm1_gain[None, :], w_qkv.reshape(1024, 256), segment_ids.reshape(4, 128))
     asked = across(ask)
@@ -570,15 +594,15 @@
     shards = [v for p in zip([pre] + far_pre, near_pre) for v in p]
     second = begin_call(asked, shards)
 
-    far_new, side, opposite, second = tie((far_new, side, opposite, second))
+    far_new, second = tie((far_new, second))
     near_new += [swap(v) for v in far_new]
-    wz = [side, swap(side), opposite]
     pays = [v for p in zip([pay] + far_new, near_new) for v in p]
     message = partner_call(asked, second, pays)
 
-    wz, near_new, message, expert_in_t, expert_out_t = tie(
-        (wz, near_new, message, expert_in, expert_out)
-    )
+    side, opposite, near_new, message, expert_in_t, expert_out_t = tie(
+        (side, opposite, near_new, message, expert_in, expert_out)
+    )
+    wz = [side, swap(side), opposite]
     returned = across(message)
     wi_peer = swap(expert_in_t)
     wo_peer = swap(expert_out_t)

time: 199 us -> 198 us (level); the launches traced: 198 us -> 200 us
  blocking collectives: 62 us -> 93.5 us
  Pallas kernels: 99 us -> 80.9 us
  starting transfers between devices: 28.7 us -> 19.4 us
  local copies, waits for them, and re-layouts: 4.65 us -> 1.94 us
    pallas_call x1, Pallas kernels: 37.1 us -> 10.5 us  [own_call(): pl.pallas_call(own_kernel, in_specs=[HBM, VM, VM, VM] + [HBM] * 14, out_s...]
    all_to_all x1, blocking collectives: 9.89 us -> 36.3 us  [body(): lax.all_to_all(attended.reshape(8, ROWS, 128), 'tp', 0, 0, tiled=True)]
    ppermute x1, starting transfers between devices: 10.6 us -> 0.09 us  [body(): opposite = lax.ppermute(wpair, 'tp', tp_perm(lambda a, b: (a, (b + 2) % 4)))]
    pallas_call x2, Pallas kernels: 45.1 us -> 53.2 us  [begin_call(): pl.pallas_call(functools.partial(begin_kernel, count=count), in_specs=[HB...]
    all_to_all x1, blocking collectives: 30.6 us -> 37.2 us  [body(): lax.all_to_all(copies, 'seq', 0, 0, axis_index_groups=CHIP_GROUPS, tiled=...]
    ppermute x1, starting transfers between devices: 0.74 us -> 3.59 us  [body(): side = lax.ppermute(wpair, ('seq', 'tp'), SIDES)]
    unnamed x27 -> x25, local copies, waits for them, and re-layouts: 4.63 us -> 1.92 us
  transfers between devices with their start and end apart: 22 -> 22, of which waited for: 4 -> 4; matrix products, arithmetic and copies ran while one was open for 0% -> 0% of each run, Pallas kernels for 46% -> 37%
where the time goes in v1:
time: 198 us; the launch traced here: 200 us
  blocking collectives  93.5 us (47%)
  Pallas kernels  80.9 us (41%)
  starting transfers between devices  19.4 us (10%)
  waiting for transfers between devices  2.61 us (1%)
    pallas_call x2, Pallas kernels, begin_call(): pl.pallas_call(functools.partial(begin_kernel, count=count), in_specs=[HB...  53.2 us
    all_to_all x1, blocking collectives, body(): lax.all_to_all(copies, 'seq', 0, 0, axis_index_groups=CHIP_GROUPS, tiled=...  37.2 us
    all_to_all x1, blocking collectives, body(): lax.all_to_all(attended.reshape(8, ROWS, 128), 'tp', 0, 0, tiled=True)  36.3 us
    all_to_all x1, blocking collectives, body(): lax.all_to_all(partial.reshape(8, ROWS, 1024), 'seq', 0, 0, axis_index_gr...  20.1 us
    pallas_call x1, Pallas kernels, own_call(): pl.pallas_call(own_kernel, in_specs=[HBM, VM, VM, VM] + [HBM] * 14, out_s...  10.5 us
    ppermute x6, starting transfers between devices, round_y(): lax.ppermute(v, 'seq', seq_perm(lambda a, b, d, k=k: (a, (b + k) % 4, d)))  8.74 us
    pallas_call x1, Pallas kernels, expert_call(): pl.pallas_call(expert_kernel, in_specs=[VM] * 5, out_specs=VM, scratch_sh...  7.44 us
    pallas_call x1, Pallas kernels, partner_call(): pl.pallas_call(partner_kernel, in_specs=[HBM, VM, VM] + [HBM] * 8, out_sp...  5.44 us
  transfers between devices with their start and end apart: 22, of which 4 were waited for; matrix products, arithmetic and copies ran while one was open for 0% of the time, Pallas kernels for 37%

profile of v1, /device:TPU:0, one launch (start us, length us, event | category | flops | bytes accessed | tf_op | source)
XLA Modules:
  0.0 200.1 jit_solution(11727710835599498202)
XLA Ops:
  0.6 0.1 collective-permute-start.4
  0.7 3.4 %collective-permute-start.2 = (bf16[1024,128]{1,0:T(8,128)(2,1)}, bf16[1024,128]{1,0:T(8,128)(2,1)S(1)}, u32[]{:S(2)}, u32[]{:S(2)}) collective-permute-start(bf16[1024,128]{1,0:T(8,128)(2,1)} %bitcast.18), channel_id=1, source_target_pairs={{0,32},{8,40},{16,48},{24,56},{32,0},{40,8},{48,16},{56,24},{64,96... | collective-permute-start | bytes 786440 | tf_op jit(solution)/shard_map/ppermute | solution.py:554
  4.1 1.1 collective-permute-start.1
  5.1 1.0 collective-permute-start
  6.1 1.5 collective-permute-start.15
  7.6 3.3 %project.1 = (bf16[528,128]{1,0:T(8,128)(2,1)}, bf16[528,128]{1,0:T(8,128)(2,1)}, f32[8,1024]{1,0:T(8,128)}, bf16[512,128]{1,0:T(8,128)(2,1)}) custom-call(bf16[512,1024]{1,0:T(8,128)(2,1)} %tok_hbm.3, f32[1,1024]{1,0:T(1,128)} %bitcast.24, bf16[1024,256]{1,0:T(8,128)(2,1)} %bitcast.23, s32[4,128]{1,0:T(4,128)} %bitcast.25), custom_call_target="tpu_custom_call" | custom-call | flops 268435456 | bytes 2097152 | tf_op jit(solution)/shard_map/project/pallas_call | solution.py:562
  10.9 0.0 copy-start.3
  10.9 2.8 %collective-permute-start.3 = (bf16[528,128]{1,0:T(8,128)(2,1)}, bf16[528,128]{1,0:T(8,128)(2,1)S(1)}, u32[]{:S(2)}, u32[]{:S(2)}) collective-permute-start(bf16[528,128]{1,0:T(8,128)(2,1)} %get-tuple-element.33.ask_hbm), channel_id=1, source_target_pairs={{0,64},{8,72},{16,80},{24,88},{32,96},{40,104},{48,112},{56,120},{... | collective-permute-start | bytes 405512 | tf_op jit(solution)/shard_map/ppermute | solution.py:550
  13.7 0.9 copy-done.7
  14.6 0.9 copy-done.10
  15.6 11.0 %attend_prefix.2 = (f32[80,1024]{1,0:T(8,128)S(1)}, f32[8,1024]{1,0:T(8,128)S(1)}) custom-call(bf16[528,128]{1,0:T(8,128)(2,1)S(1)} %copy-done.10, bf16[1024,128]{1,0:T(8,128)(2,1)S(1)} %bitcast.21, bf16[1024,128]{1,0:T(8,128)(2,1)S(1)} %collective-permute-done.4.refs_1_), custom_call_target="tpu_custom_call" | custom-call | flops 2516582400 | bytes 524288 | tf_op jit(solution)/shard_map/attend_prefix/pallas_call | solution.py:287
  26.6 0.0 collective-permute-done.2.refs_6_.refs_4_
  26.6 0.0 collective-permute-done.1.refs_4_.refs_2_
  26.6 0.1 collective-permute-start.5
  26.7 0.5 collective-permute-start.6
  27.2 0.1 collective-permute-start.7
  27.3 0.4 collective-permute-start.8
  27.7 0.0 collective-permute-done.15.w1
  27.8 0.1 collective-permute-start.17
  27.8 1.3 collective-permute-done.8.refs_7_.refs_1_
  29.1 3.6 %collective-permute-start.16 = (bf16[2,128,1024]{2,1,0:T(8,128)(2,1)S(1)}, bf16[2,128,1024]{2,1,0:T(8,128)(2,1)S(1)}, u32[]{:S(2)}, u32[]{:S(2)}) collective-permute-start(bf16[2,128,1024]{2,1,0:T(8,128)(2,1)S(1)} %constant_dynamic-update-slice_fusion), channel_id=1, source_target_pairs={{0,1},{1,2},{2,3},{3,0},{4,5},{5,6},{6,7},{7,4},{8,11},{9,8},{10,9... | collective-permute-start | bytes 1572872 | tf_op jit(solution)/shard_map/ppermute | solution.py:592
  32.7 0.0 collective-permute-done.5.refs_3_.refs_1_
  32.7 0.7 collective-permute-start.11
  33.5 2.6 %collective-permute-start.10 = (bf16[528,128]{1,0:T(8,128)(2,1)S(1)}, bf16[528,128]{1,0:T(8,128)(2,1)S(1)}, u32[]{:S(2)}, u32[]{:S(2)}) collective-permute-start(bf16[528,128]{1,0:T(8,128)(2,1)S(1)} %copy-done.9), channel_id=1, source_target_pairs={{0,48},{8,56},{16,0},{24,8},{32,16},{40,24},{48,32},{56,40},{64,11... | collective-permute-start | bytes 405512 | tf_op jit(solution)/shard_map/ppermute | solution.py:554
  36.1 42.3 %attend_prefix.3 = (f32[80,1024]{1,0:T(8,128)S(1)}, f32[8,1024]{1,0:T(8,128)S(1)}) custom-call(bf16[528,128]{1,0:T(8,128)(2,1)S(1)} %collective-permute-done.3.ask_hbm, bf16[1024,128]{1,0:T(8,128)(2,1)S(1)} %bitcast.22, bf16[1024,128]{1,0:T(8,128)(2,1)S(1)} %collective-permute-done.4.refs_1_, bf16[1024,128]{1,0:T(8,128)(2,1)S(1)} %collective-permute-done.refs_2_.refs_0_, ...), custom_call_target="tpu_custom_call" | custom-call | flops 10066329600 | bytes 2097152 | tf_op jit(solution)/shard_map/attend_prefix/pallas_call | solution.py:287
  78.4 0.0 copy-start
  78.4 0.0 copy-start.2
  78.4 0.0 copy-start.11
  78.5 0.1 collective-permute-start.12
  78.5 0.5 collective-permute-start.13
  79.0 0.1 collective-permute-start.14
  79.1 0.7 collective-permute-done.12.refs_9_.refs_3_
  79.9 0.2 collective-permute-done.13.refs_11_.refs_5_
  80.1 0.3 collective-permute-done.14.refs_13_.refs_7_
  80.4 5.4 %attend_partner.1 = f32[72,1024]{1,0:T(8,128)S(1)} custom-call(bf16[528,128]{1,0:T(8,128)(2,1)S(1)} %collective-permute-done.3.ask_hbm, f32[80,1024]{1,0:T(8,128)S(1)} %get-tuple-element.54.o_in, f32[8,1024]{1,0:T(8,128)S(1)} %get-tuple-element.55.m_in, bf16[528,128]{1,0:T(8,128)(2,1)S(1)} %copy-done.9, ...), custom_call_target="tpu_custom_call" | custom-call | flops 1887436800 | bytes 393216 | tf_op jit(solution)/shard_map/attend_partner/pallas_call | solution.py:346
  85.9 0.3 collective-permute-start.20
  86.2 0.3 collective-permute-start.19
  86.5 0.2 collective-permute-start.21
  86.7 0.0 copy-start.6
  86.7 10.5 %attend_own.1 = (f32[80,1024]{1,0:T(8,128)S(1)}, f32[8,1024]{1,0:T(8,128)S(1)}) custom-call(bf16[528,128]{1,0:T(8,128)(2,1)S(1)} %copy-done.10, f32[8,1024]{1,0:T(8,128)S(1)} %copy-done.11, f32[80,1024]{1,0:T(8,128)S(1)} %get-tuple-element.38.o_in, f32[8,1024]{1,0:T(8,128)S(1)} %get-tuple-element.39.m_in, ...), custom_call_target="tpu_custom_call" | custom-call | flops 11324620800 | bytes 2359296 | tf_op jit(solution)/shard_map/attend_own/pallas_call | solution.py:406
  97.2 0.1 join.1
  97.4 36.3 %all_to_all.15.att_ref = bf16[8,64,128]{2,1,0:T(8,128)(2,1)S(1)} all-to-all(bf16[8,64,128]{2,1,0:T(8,128)(2,1)S(1)} %bitcast.13), channel_id=1, replica_groups=mesh['seq'=16,'tp'=8] {'tp'}, dimensions={0} | all-to-all | bytes 262144 | tf_op jit(solution)/shard_map/all_to_all | solution.py:614
  133.6 0.9 mix.1
  134.5 37.2 %all_to_all.16 = bf16[8,64,1152]{2,1,0:T(8,128)(2,1)S(1)} all-to-all(bf16[8,64,1152]{2,1,0:T(8,128)(2,1)S(1)} %get-tuple-element.60), channel_id=1, replica_groups={{0,16,32,48,64,80,96,112},{8,24,40,56,72,88,104,120},{1,17,33,49,65,81,..., dimensions={0} | all-to-all | bytes 2359296 | tf_op jit(solution)/shard_map/all_to_all | solution.py:623
  171.7 7.4 %experts.1 = bf16[512,1024]{1,0:T(8,128)(2,1)S(1)} custom-call(bf16[512,1152]{1,0:T(8,128)(2,1)S(1)} %bitcast.11, bf16[2,1024,1024]{2,1,0:T(8,128)(2,1)S(1)} %copy-done, bf16[2,1024,1024]{2,1,0:T(8,128)(2,1)S(1)} %collective-permute-done.20.wi_peer, bf16[2,512,1024]{2,1,0:T(8,128)(2,1)S(1)} %copy-done.2, ...), custom_call_target="tpu_custom_call" | custom-call | tf_op jit(solution)/shard_map/experts/pallas_call | solution.py:517
  179.1 20.1 %all_to_all.17 = bf16[8,64,1024]{2,1,0:T(8,128)(2,1)S(1)} all-to-all(bf16[8,64,1024]{2,1,0:T(8,128)(2,1)S(1)} %bitcast.12), channel_id=1, replica_groups={{0,16,32,48,64,80,96,112},{8,24,40,56,72,88,104,120},{1,17,33,49,65,81,..., dimensions={0} | all-to-all | bytes 2097152 | tf_op jit(solution)/shard_map/all_to_all | solution.py:627
  199.2 0.2 convert_reduce_fusion
  199.4 0.7 add_convert_fusion
  (35 shorter events, 0.1 us)
Async XLA Ops:
  0.6 10.2 %collective-permute-start.4 = (bf16[1024,128]{1,0:T(8,128)(2,1)}, bf16[1024,128]{1,0:T(8,128)(2,1)S(1)}, u32[]{:S(2)}, u32[]{:S(2)}) collective-permute-start(bf16[1024,128]{1,0:T(8,128)(2,1)} %bitcast.17), channel_id=1, source_target_pairs={{0,8},{8,0},{16,24},{24,16},{32,40},{40,32},{48,56},{56,48},{64,72... | collective-permute-start | bytes 786440 | tf_op jit(solution)/shard_map/ppermute | solution.py:547
  0.7 25.8 %collective-permute-start.2 = (bf16[1024,128]{1,0:T(8,128)(2,1)}, bf16[1024,128]{1,0:T(8,128)(2,1)S(1)}, u32[]{:S(2)}, u32[]{:S(2)}) collective-permute-start(bf16[1024,128]{1,0:T(8,128)(2,1)} %bitcast.18), channel_id=1, source_target_pairs={{0,32},{8,40},{16,48},{24,56},{32,0},{40,8},{48,16},{56,24},{64,96... | collective-permute-start | bytes 786440 | tf_op jit(solution)/shard_map/ppermute | solution.py:554
  4.1 22.5 %collective-permute-start.1 = (bf16[1024,128]{1,0:T(8,128)(2,1)}, bf16[1024,128]{1,0:T(8,128)(2,1)S(1)}, u32[]{:S(2)}, u32[]{:S(2)}) collective-permute-start(bf16[1024,128]{1,0:T(8,128)(2,1)} %bitcast.19), channel_id=1, source_target_pairs={{0,48},{8,56},{16,0},{24,8},{32,16},{40,24},{48,32},{56,40},{64,11... | collective-permute-start | bytes 786440 | tf_op jit(solution)/shard_map/ppermute | solution.py:554
  5.1 21.4 %collective-permute-start = (bf16[1024,128]{1,0:T(8,128)(2,1)}, bf16[1024,128]{1,0:T(8,128)(2,1)S(1)}, u32[]{:S(2)}, u32[]{:S(2)}) collective-permute-start(bf16[1024,128]{1,0:T(8,128)(2,1)} %bitcast.20), channel_id=1, source_target_pairs={{0,16},{8,24},{16,32},{24,40},{32,48},{40,56},{48,0},{56,8},{64,80... | collective-permute-start | bytes 786440 | tf_op jit(solution)/shard_map/ppermute | solution.py:554
  6.1 21.6 %collective-permute-start.15 = (bf16[1,128,1024]{2,1,0:T(8,128)(2,1)}, bf16[1,128,1024]{2,1,0:T(8,128)(2,1)S(1)}, u32[]{:S(2)}, u32[]{:S(2)}) collective-permute-start(bf16[1,128,1024]{2,1,0:T(8,128)(2,1)} %w0.1), channel_id=1, source_target_pairs={{0,4},{1,5},{2,6},{3,7},{4,0},{5,1},{6,2},{7,3},{8,12},{9,13},{10,... | collective-permute-start | bytes 786440 | tf_op jit(solution)/shard_map/ppermute | solution.py:559
  10.9 16.8 %copy-start.3 = (bf16[1,128,1024]{2,1,0:T(8,128)(2,1)S(1)}, bf16[1,128,1024]{2,1,0:T(8,128)(2,1)}, u32[]{:S(2)}) copy-start(bf16[1,128,1024]{2,1,0:T(8,128)(2,1)} %w0.1) | copy-start | bytes 786436
  10.9 15.7 %collective-permute-start.3 = (bf16[528,128]{1,0:T(8,128)(2,1)}, bf16[528,128]{1,0:T(8,128)(2,1)S(1)}, u32[]{:S(2)}, u32[]{:S(2)}) collective-permute-start(bf16[528,128]{1,0:T(8,128)(2,1)} %get-tuple-element.33.ask_hbm), channel_id=1, source_target_pairs={{0,64},{8,72},{16,80},{24,88},{32,96},{40,104},{48,112},{56,120},{... | collective-permute-start | bytes 405512 | tf_op jit(solution)/shard_map/ppermute | solution.py:550
  13.7 0.9 copy-start.7
  14.6 0.9 copy-start.10
  15.6 11.7 %copy-start.9 = (bf16[528,128]{1,0:T(8,128)(2,1)S(1)}, bf16[528,128]{1,0:T(8,128)(2,1)}, u32[]{:S(2)}) copy-start(bf16[528,128]{1,0:T(8,128)(2,1)} %get-tuple-element.44.refs_6_.refs_0_) | copy-start | bytes 405508
  15.6 20.5 %copy-start.8 = (bf16[1024,1,128]{2,0,1:T(8,128)(2,1)S(1)}, bf16[1024,1,128]{2,0,1:T(8,128)(2,1)}, u32[]{:S(2)}) copy-start(bf16[1024,1,128]{2,0,1:T(8,128)(2,1)} %param.13) | copy-start | bytes 786436
  26.6 6.2 %collective-permute-start.5 = (bf16[1024,128]{1,0:T(8,128)(2,1)S(1)}, bf16[1024,128]{1,0:T(8,128)(2,1)S(1)}, u32[]{:S(2)}, u32[]{:S(2)}) collective-permute-start(bf16[1024,128]{1,0:T(8,128)(2,1)S(1)} %collective-permute-done.refs_2_.refs_0_), channel_id=1, source_target_pairs={{0,8},{8,0},{16,24},{24,16},{32,40},{40,32},{48,56},{56,48},{64,72... | collective-permute-start | bytes 786440 | tf_op jit(solution)/shard_map/ppermute | solution.py:547
  26.7 6.8 %collective-permute-start.6 = (bf16[1024,128]{1,0:T(8,128)(2,1)S(1)}, bf16[1024,128]{1,0:T(8,128)(2,1)S(1)}, u32[]{:S(2)}, u32[]{:S(2)}) collective-permute-start(bf16[1024,128]{1,0:T(8,128)(2,1)S(1)} %collective-permute-done.1.refs_4_.refs_2_), channel_id=1, source_target_pairs={{0,8},{8,0},{16,24},{24,16},{32,40},{40,32},{48,56},{56,48},{64,72... | collective-permute-start | bytes 786440 | tf_op jit(solution)/shard_map/ppermute | solution.py:547
  27.2 8.9 %collective-permute-start.7 = (bf16[1024,128]{1,0:T(8,128)(2,1)S(1)}, bf16[1024,128]{1,0:T(8,128)(2,1)S(1)}, u32[]{:S(2)}, u32[]{:S(2)}) collective-permute-start(bf16[1024,128]{1,0:T(8,128)(2,1)S(1)} %collective-permute-done.2.refs_6_.refs_4_), channel_id=1, source_target_pairs={{0,8},{8,0},{16,24},{24,16},{32,40},{40,32},{48,56},{56,48},{64,72... | collective-permute-start | bytes 786440 | tf_op jit(solution)/shard_map/ppermute | solution.py:547
  27.3 1.9 collective-permute-start.8
  27.8 58.1 %collective-permute-start.17 = (bf16[2,128,1024]{2,1,0:T(8,128)(2,1)S(1)}, bf16[2,128,1024]{2,1,0:T(8,128)(2,1)S(1)}, u32[]{:S(2)}, u32[]{:S(2)}) collective-permute-start(bf16[2,128,1024]{2,1,0:T(8,128)(2,1)S(1)} %constant_dynamic-update-slice_fusion), channel_id=1, source_target_pairs={{0,2},{1,3},{2,0},{3,1},{4,6},{5,7},{6,4},{7,5},{8,10},{9,11},{10,... | collective-permute-start | bytes 1572872 | tf_op jit(solution)/shard_map/ppermute | solution.py:593
  29.1 56.7 %collective-permute-start.16 = (bf16[2,128,1024]{2,1,0:T(8,128)(2,1)S(1)}, bf16[2,128,1024]{2,1,0:T(8,128)(2,1)S(1)}, u32[]{:S(2)}, u32[]{:S(2)}) collective-permute-start(bf16[2,128,1024]{2,1,0:T(8,128)(2,1)S(1)} %constant_dynamic-update-slice_fusion), channel_id=1, source_target_pairs={{0,1},{1,2},{2,3},{3,0},{4,5},{5,6},{6,7},{7,4},{8,11},{9,8},{10,9... | collective-permute-start | bytes 1572872 | tf_op jit(solution)/shard_map/ppermute | solution.py:592
  32.7 45.6 %collective-permute-start.11 = (bf16[528,128]{1,0:T(8,128)(2,1)S(1)}, bf16[528,128]{1,0:T(8,128)(2,1)S(1)}, u32[]{:S(2)}, u32[]{:S(2)}) collective-permute-start(bf16[528,128]{1,0:T(8,128)(2,1)S(1)} %copy-done.9), channel_id=1, source_target_pairs={{0,32},{8,40},{16,48},{24,56},{32,0},{40,8},{48,16},{56,24},{64,96... | collective-permute-start | bytes 405512 | tf_op jit(solution)/shard_map/ppermute | solution.py:554
  33.5 44.9 %collective-permute-start.10 = (bf16[528,128]{1,0:T(8,128)(2,1)S(1)}, bf16[528,128]{1,0:T(8,128)(2,1)S(1)}, u32[]{:S(2)}, u32[]{:S(2)}) collective-permute-start(bf16[528,128]{1,0:T(8,128)(2,1)S(1)} %copy-done.9), channel_id=1, source_target_pairs={{0,48},{8,56},{16,0},{24,8},{32,16},{40,24},{48,32},{56,40},{64,11... | collective-permute-start | bytes 405512 | tf_op jit(solution)/shard_map/ppermute | solution.py:554
  36.1 42.3 %collective-permute-start.9 = (bf16[528,128]{1,0:T(8,128)(2,1)S(1)}, bf16[528,128]{1,0:T(8,128)(2,1)S(1)}, u32[]{:S(2)}, u32[]{:S(2)}) collective-permute-start(bf16[528,128]{1,0:T(8,128)(2,1)S(1)} %copy-done.9), channel_id=1, source_target_pairs={{0,16},{8,24},{16,32},{24,40},{32,48},{40,56},{48,0},{56,8},{64,80... | collective-permute-start | bytes 405512 | tf_op jit(solution)/shard_map/ppermute | solution.py:554
  78.4 7.5 %copy-start = (bf16[2,1024,1024]{2,1,0:T(8,128)(2,1)S(1)}, bf16[2,1024,1024]{2,1,0:T(8,128)(2,1)}, u32[]{:S(2)}) copy-start(bf16[2,1024,1024]{2,1,0:T(8,128)(2,1)} %wi_own.1) | copy-start | bytes 12582916
  78.4 8.0 %copy-start.2 = (bf16[2,512,1024]{2,1,0:T(8,128)(2,1)S(1)}, bf16[2,512,1024]{2,1,0:T(8,128)(2,1)}, u32[]{:S(2)}) copy-start(bf16[2,512,1024]{2,1,0:T(8,128)(2,1)} %wo_own.1) | copy-start | bytes 6291460
  78.4 8.2 %copy-start.11 = (f32[8,1024]{1,0:T(8,128)S(1)}, f32[8,1024]{1,0:T(8,128)}, u32[]{:S(2)}) copy-start(f32[8,1024]{1,0:T(8,128)} %get-tuple-element.34.row_ref) | copy-start | bytes 98308
  78.5 1.4 collective-permute-start.12
  78.5 1.5 collective-permute-start.13
  79.0 1.4 collective-permute-start.14
  85.9 85.8 %collective-permute-start.20 = (bf16[2,1024,1024]{2,1,0:T(8,128)(2,1)S(1)}, bf16[2,1024,1024]{2,1,0:T(8,128)(2,1)S(1)}, u32[]{:S(2)}, u32[]{:S(2)}) collective-permute-start(bf16[2,1024,1024]{2,1,0:T(8,128)(2,1)S(1)} %copy-done), channel_id=1, source_target_pairs={{0,8},{8,0},{16,24},{24,16},{32,40},{40,32},{48,56},{56,48},{64,72... | collective-permute-start | bytes 12582920 | tf_op jit(solution)/shard_map/ppermute | solution.py:547
  86.2 11.1 %collective-permute-start.18 = (f32[72,1024]{1,0:T(8,128)S(1)}, f32[72,1024]{1,0:T(8,128)S(1)}, u32[]{:S(2)}, u32[]{:S(2)}) collective-permute-start(f32[72,1024]{1,0:T(8,128)S(1)} %attend_partner.1), channel_id=1, source_target_pairs={{0,64},{8,72},{16,80},{24,88},{32,96},{40,104},{48,112},{56,120},{... | collective-permute-start | bytes 884744 | tf_op jit(solution)/shard_map/ppermute | solution.py:550
  86.2 47.5 %collective-permute-start.19 = (bf16[2,128,1024]{2,1,0:T(8,128)(2,1)S(1)}, bf16[2,128,1024]{2,1,0:T(8,128)(2,1)S(1)}, u32[]{:S(2)}, u32[]{:S(2)}) collective-permute-start(bf16[2,128,1024]{2,1,0:T(8,128)(2,1)S(1)} %collective-permute-done.16.w2), channel_id=1, source_target_pairs={{0,8},{8,0},{16,24},{24,16},{32,40},{40,32},{48,56},{56,48},{64,72... | collective-permute-start | bytes 1572872 | tf_op jit(solution)/shard_map/ppermute | solution.py:547
  86.5 85.2 %collective-permute-start.21 = (bf16[2,512,1024]{2,1,0:T(8,128)(2,1)S(1)}, bf16[2,512,1024]{2,1,0:T(8,128)(2,1)S(1)}, u32[]{:S(2)}, u32[]{:S(2)}) collective-permute-start(bf16[2,512,1024]{2,1,0:T(8,128)(2,1)S(1)} %copy-done.2), channel_id=1, source_target_pairs={{0,8},{8,0},{16,24},{24,16},{32,40},{40,32},{48,56},{56,48},{64,72... | collective-permute-start | bytes 6291464 | tf_op jit(solution)/shard_map/ppermute | solution.py:547
  86.7 46.9 %copy-start.1 = (bf16[512,1024]{1,0:T(8,128)(2,1)S(1)}, bf16[512,1024]{1,0:T(8,128)(2,1)}, u32[]{:S(2)}) copy-start(bf16[512,1024]{1,0:T(8,128)(2,1)} %tok_hbm.3) | copy-start | bytes 3145732
  86.7 46.9 %copy-start.4 = (f32[1024]{0:T(1024)S(1)}, f32[1024]{0:T(1024)}, u32[]{:S(2)}) copy-start(f32[1024]{0:T(1024)} %param.17) | copy-start | bytes 12292
  86.7 47.0 %copy-start.5 = (s32[64,8]{0,1:T(8,128)S(1)}, s32[64,8]{0,1:T(8,128)}, u32[]{:S(2)}) copy-start(s32[64,8]{0,1:T(8,128)} %param.20) | copy-start | bytes 6148
  86.7 47.0 %copy-start.6 = (f32[64,8]{0,1:T(8,128)S(1)}, f32[64,8]{0,1:T(8,128)}, u32[]{:S(2)}) copy-start(f32[64,8]{0,1:T(8,128)} %param.21) | copy-start | bytes 6148

commit v2 on v1

--- a/solution.py
+++ b/solution.py
@@ -193,8 +193,7 @@
         add_block(buf[pl.ds(at, size), :], q_ref, o_ref, m_ref, mask, level)
 
     pl.when(low < end)(lambda: block(low * TD, TD, "start"))
-    if diagonal:
-        block(end * TD, TD, "both")
+    pl.when(diagonal)(lambda: block(end * TD, TD, "both"))
     between = jnp.maximum(end - 1 - low, 0)
     split = lax.rem(between, 2)
     pl.when(split == 1)(lambda: block((low + 1) * TD, TD, None, 1))
@@ -297,57 +296,97 @@
     )(ask, *parts)
 
 
-def partner_kernel(ask_hbm, o_in, m_in, *refs):
+def own_terms(row_ref, segs, own):
+    row = row_ref[1:2, :]
+    mine = jnp.max(jnp.where(lax.broadcasted_iota(jnp.int32, (1, NQ), 1) == 0, row, -1.0))
+    begin = own * TD - count_same(segs, mine, [v < own for v in half_sources()])
+    start = jnp.where(row == mine, begin, row_ref[0:1, :].astype(jnp.int32) + own * TD)
+    lane = lax.broadcasted_iota(jnp.int32, (1, NQ), 1)
+    last = own * TD + jnp.where(lane >= TD, lane - TD, lane)
+    return start, last, jnp.where(row == mine, 1, 0), begin // TD
+
+
+def partner_terms(marks, segs):
+    newest = segs[0].astype(F32)
+    for j in range(1, 8):
+        newest = jnp.maximum(newest, segs[j].astype(F32))
+    newest = jnp.max(newest)
+    begin = 8 * TD - count_same(segs, newest, [True] * 8)
+    seg = marks[...].astype(F32)
+    row = jnp.concatenate([seg[k : k + 1, :] for k in range(4)], axis=1)
+    row = jnp.concatenate([row, row], axis=1)
+    start = jnp.where(row == newest, begin, 8 * TD)
+    last = jnp.full((1, NQ), 8 * TD, jnp.int32)
+    return start, last, jnp.where(row == newest, 1, 0), jnp.min(start) // TD
+
+
+def partner_kernel(ask_hbm, own_hbm, row_ref, o_in, m_in, o_own, m_own, *refs):
     pays = refs[:8]
-    out_ref, stage, marks, q_ref, o_ref, m_ref, buf, segs, sem = refs[8:]
-    o_ref[...] = o_in[...]
-    m_ref[...] = m_in[...]
-
-    @pl.when(place()[0] == 0)
-    def _():
-        copies = fetch_all(
-            news_pairs(pays, buf, segs)
-            + [
-                (ask_hbm.at[pl.ds(0, TD), :], stage),
-                (ask_hbm.at[pl.ds(SEG_AT, 16), :], marks),
-            ],
-            sem,
-        )
-        for v in copies[:8] + copies[16:]:
-            v.wait()
-        spread_heads(stage, q_ref)
-        newest = segs[0].astype(F32)
-        for j in range(1, 8):
-            newest = jnp.maximum(newest, segs[j].astype(F32))
-        newest = jnp.max(newest)
-        begin = 8 * TD - count_same(segs, newest, [True] * 8)
-        seg = marks[...].astype(F32)
-        row = jnp.concatenate([seg[k : k + 1, :] for k in range(4)], axis=1)
-        row = jnp.concatenate([row, row], axis=1)
-        start = jnp.where(row == newest, begin, 8 * TD)
-        last = jnp.full((1, NQ), 8 * TD, jnp.int32)
-        low = jnp.min(start) // TD
-        for v in copies[8:16]:
-            v.wait()
-        add_suffix(low, 8, False, start, None, row == newest, buf, q_ref, o_ref, m_ref)
-
-        @pl.when(too_large(o_ref))
+    out_ref, o_out, m_out, stage, marks, q_ref, o_ref, m_ref, buf, segs, sem = refs[8:]
+    x, y, c = place()
+    own = y * 2 + c
+    early = x == 0
+    asked = pltpu.make_async_copy(ask_hbm.at[pl.ds(0, TD), :], stage, sem.at[17])
+    mine = pltpu.make_async_copy(own_hbm.at[pl.ds(0, TD), :], stage, sem.at[17])
+    pl.when(early)(lambda: asked.start())
+    pl.when(jnp.logical_not(early))(lambda: mine.start())
+    copies = fetch_all(
+        news_pairs(pays, buf, segs) + [(ask_hbm.at[pl.ds(SEG_AT, 16), :], marks)], sem
+    )
+
+    def load():
+        @pl.when(early)
         def _():
             o_ref[...] = o_in[...]
             m_ref[...] = m_in[...]
-            again_suffix(low, 8, start, last, buf, q_ref, o_ref, m_ref)
-
-    out_ref[:HD, :] = o_ref[:HD, :]
+
+        @pl.when(jnp.logical_not(early))
+        def _():
+            o_ref[...] = o_own[...]
+            m_ref[...] = m_own[...]
+
+    load()
+    for v in copies[:8] + copies[16:]:
+        v.wait()
+    asked.wait()
+    spread_heads(stage, q_ref)
+    theirs, ours = partner_terms(marks, segs), own_terms(row_ref, segs, own)
+    start, last, reach, low = [jnp.where(early, a, b) for a, b in zip(theirs, ours)]
+    end = jnp.where(early, 8, own)
+    for v in copies[8:16]:
+        v.wait()
+    add_suffix(low, end, x == 1, start, last, reach == 1, buf, q_ref, o_ref, m_ref)
+
+    @pl.when(too_large(o_ref))
+    def _():
+        load()
+        again_suffix(low, end + x, start, last, buf, q_ref, o_ref, m_ref)
+
     first = lax.broadcasted_iota(jnp.int32, (8, NQ), 0) == 0
-    out_ref[HD:, :] = jnp.where(first, o_ref[HD : HD + 1, :], m_ref[0:1, :])
-
-
-def partner_call(ask, state, pays):
+
+    def tell(o, m):
+        out_ref[:HD, :] = o[:HD, :]
+        out_ref[HD:, :] = jnp.where(first, o[HD : HD + 1, :], m[0:1, :])
+
+    @pl.when(early)
+    def _():
+        tell(o_ref, m_ref)
+        o_out[...] = o_own[...]
+        m_out[...] = m_own[...]
+
+    @pl.when(jnp.logical_not(early))
+    def _():
+        tell(o_in, m_in)
+        o_out[...] = o_ref[...]
+        m_out[...] = m_ref[...]
+
+
+def partner_call(ask, own_ask, rows, state, own_state, pays):
     return pl.pallas_call(
         partner_kernel,
-        in_specs=[HBM, VM, VM] + [HBM] * 8,
-        out_specs=VM,
-        out_shape=jax.ShapeDtypeStruct((MSG, NQ), F32),
+        in_specs=[HBM, HBM] + [VM] * 5 + [HBM] * 8,
+        out_specs=[VM] * 3,
+        out_shape=[jax.ShapeDtypeStruct((MSG, NQ), F32)] + STATE,
         scratch_shapes=[
             ASK[0],
             pltpu.VMEM((16, 128), BF),
@@ -361,7 +400,7 @@
         cost_estimate=price(3 * TD),
         compiler_params=room(20),
         name="attend_partner",
-    )(ask, state[0], state[1], *pays)
+    )(ask, own_ask, rows, *state, *own_state, *pays)
 
 
 def own_kernel(ask_hbm, row_ref, o_in, m_in, *refs):
@@ -369,34 +408,43 @@
     pays = refs[6:14]
     out_ref, top_ref, stage, q_ref, o_ref, m_ref, pre, buf, segs, sem, pre_sem = refs[14:]
     x, y, c = place()
+    own = y * 2 + c
     asked = pltpu.make_async_copy(ask_hbm.at[pl.ds(0, TD), :], stage, sem.at[16])
     asked.start()
     fetch_all([(parts[j], pre.at[j]) for j in range(6)], pre_sem)
-    copies = fetch_all(news_pairs(pays, buf, segs), sem)
+    copies = [
+        pltpu.make_async_copy(a, b, sem.at[i])
+        for i, (a, b) in enumerate(news_pairs(pays, buf, segs))
+    ]
+
+    @pl.when(x == 0)
+    def _():
+        for v in copies:
+            v.start()
+
     o_ref[...] = o_in[...]
     m_ref[...] = m_in[...]
     asked.wait()
     spread_heads(stage, q_ref)
     add_prefix(6, pre, pre_sem, q_ref, o_ref, m_ref, False)
-    for v in copies:
-        v.wait()
-    own = y * 2 + c
-    row = row_ref[1:2, :]
-    mine = jnp.max(jnp.where(lax.broadcasted_iota(jnp.int32, (1, NQ), 1) == 0, row, -1.0))
-    src = half_sources()
-    begin = own * TD - count_same(segs, mine, [v < own for v in src])
-    start = jnp.where(row == mine, begin, row_ref[0:1, :].astype(jnp.int32) + own * TD)
-    lane = lax.broadcasted_iota(jnp.int32, (1, NQ), 1)
-    last = own * TD + jnp.where(lane >= TD, lane - TD, lane)
-    low = begin // TD
-    add_suffix(low, own, True, start, last, row == mine, buf, q_ref, o_ref, m_ref)
+
+    @pl.when(x == 0)
+    def _():
+        for v in copies:
+            v.wait()
+        start, last, reach, low = own_terms(row_ref, segs, own)
+        add_suffix(low, own, x == 0, start, last, reach == 1, buf, q_ref, o_ref, m_ref)
 
     @pl.when(too_large(o_ref))
     def _():
         o_ref[...] = o_in[...]
         m_ref[...] = m_in[...]
         again_prefix(6, pre, q_ref, o_ref, m_ref)
-        again_suffix(low, own + 1, start, last, buf, q_ref, o_ref, m_ref)
+
+        @pl.when(x == 0)
+        def _():
+            start, last, reach, low = own_terms(row_ref, segs, own)
+            again_suffix(low, own + 1, start, last, buf, q_ref, o_ref, m_ref)
 
     out_ref[...] = o_ref[...]
     top_ref[...] = m_ref[...]
@@ -597,10 +645,10 @@
     far_new, second = tie((far_new, second))
     near_new += [swap(v) for v in far_new]
     pays = [v for p in zip([pay] + far_new, near_new) for v in p]
-    message = partner_call(asked, second, pays)
-
-    side, opposite, near_new, message, expert_in_t, expert_out_t = tie(
-        (side, opposite, near_new, message, expert_in, expert_out)
+    message, *first = partner_call(asked, ask, rows, second, first, pays)
+
+    side, opposite, near_new, message, first, expert_in_t, expert_out_t = tie(
+        (side, opposite, near_new, message, first, expert_in, expert_out)
     )
     wz = [side, swap(side), opposite]
     returned = across(message)

time: 198 us -> 203 us (1.025)
  Pallas kernels: 80.9 us -> 110 us
  blocking collectives: 93.5 us -> 67.8 us
    all_to_all x1, blocking collectives: 36.3 us -> 9.55 us  [body(): lax.all_to_all(attended.reshape(8, ROWS, 128), 'tp', 0, 0, tiled=True)]
    pallas_call x1, Pallas kernels: 10.5 us -> 37 us  [own_call(): pl.pallas_call(own_kernel, in_specs=[HBM, VM, VM, VM] + [HBM] * 14, out_s...]
    ppermute x1, starting transfers between devices: 0.09 us -> 3.96 us  [body(): opposite = lax.ppermute(wpair, 'tp', tp_perm(lambda a, b: (a, (b + 2) % 4)))]
    ppermute x1, starting transfers between devices: 3.59 us -> 0.01 us  [body(): side = lax.ppermute(wpair, ('seq', 'tp'), SIDES)]
    pallas_call x1, Pallas kernels: 5.44 us -> 8.09 us  [partner_call(): pl.pallas_call(partner_kernel, in_specs=[HBM, HBM] + [VM] * 5 + [HBM] * 8...]
  transfers between devices with their start and end apart: 22 -> 22, of which waited for: 4 -> 3; matrix products, arithmetic and copies ran while one was open for 0% -> 0% of each run, Pallas kernels for 37% -> 50%
where the time goes in v2:
time: 203 us
  Pallas kernels  110 us (54%)
  blocking collectives  67.8 us (33%)
  starting transfers between devices  20.7 us (10%)
    pallas_call x2, Pallas kernels, begin_call(): pl.pallas_call(functools.partial(begin_kernel, count=count), in_specs=[HB...  53.2 us
    all_to_all x1, blocking collectives, body(): lax.all_to_all(copies, 'seq', 0, 0, axis_index_groups=CHIP_GROUPS, tiled=...  38.2 us
    pallas_call x1, Pallas kernels, own_call(): pl.pallas_call(own_kernel, in_specs=[HBM, VM, VM, VM] + [HBM] * 14, out_s...  37 us
    all_to_all x1, blocking collectives, body(): lax.all_to_all(partial.reshape(8, ROWS, 1024), 'seq', 0, 0, axis_index_gr...  20 us
    ppermute x6, starting transfers between devices, round_y(): lax.ppermute(v, 'seq', seq_perm(lambda a, b, d, k=k: (a, (b + k) % 4, d)))  9.75 us
    all_to_all x1, blocking collectives, body(): lax.all_to_all(attended.reshape(8, ROWS, 128), 'tp', 0, 0, tiled=True)  9.55 us
    pallas_call x1, Pallas kernels, partner_call(): pl.pallas_call(partner_kernel, in_specs=[HBM, HBM] + [VM] * 5 + [HBM] * 8...  8.09 us
    pallas_call x1, Pallas kernels, expert_call(): pl.pallas_call(expert_kernel, in_specs=[VM] * 5, out_specs=VM, scratch_sh...  7.43 us
  transfers between devices with their start and end apart: 22, of which 3 were waited for; matrix products, arithmetic and copies ran while one was open for 0% of the time, Pallas kernels for 50%

profile of v2, /device:TPU:0, one launch (start us, length us, event | category | flops | bytes accessed | tf_op | source)
XLA Modules:
  0.0 203.5 jit_solution(15069407954967489175)
XLA Ops:
  0.6 0.1 collective-permute-start.7
  0.7 3.4 %collective-permute-start.5 = (bf16[1024,128]{1,0:T(8,128)(2,1)}, bf16[1024,128]{1,0:T(8,128)(2,1)S(1)}, u32[]{:S(2)}, u32[]{:S(2)}) collective-permute-start(bf16[1024,128]{1,0:T(8,128)(2,1)} %bitcast.18), channel_id=1, source_target_pairs={{0,32},{8,40},{16,48},{24,56},{32,0},{40,8},{48,16},{56,24},{64,96... | collective-permute-start | bytes 786440 | tf_op jit(solution)/shard_map/ppermute | solution.py:602
  4.1 1.1 collective-permute-start.4
  5.1 1.0 collective-permute-start.3
  6.1 1.5 collective-permute-start
  7.6 3.3 %project.1 = (bf16[528,128]{1,0:T(8,128)(2,1)}, bf16[528,128]{1,0:T(8,128)(2,1)}, f32[8,1024]{1,0:T(8,128)}, bf16[512,128]{1,0:T(8,128)(2,1)}) custom-call(bf16[512,1024]{1,0:T(8,128)(2,1)} %tok_hbm.3, f32[1,1024]{1,0:T(1,128)} %bitcast.24, bf16[1024,256]{1,0:T(8,128)(2,1)} %bitcast.23, s32[4,128]{1,0:T(4,128)} %bitcast.25), custom_call_target="tpu_custom_call" | custom-call | flops 268435456 | bytes 2097152 | tf_op jit(solution)/shard_map/project/pallas_call | solution.py:610
  10.9 0.0 copy-start.3
  10.9 2.8 %collective-permute-start.6 = (bf16[528,128]{1,0:T(8,128)(2,1)}, bf16[528,128]{1,0:T(8,128)(2,1)S(1)}, u32[]{:S(2)}, u32[]{:S(2)}) collective-permute-start(bf16[528,128]{1,0:T(8,128)(2,1)} %get-tuple-element.38.ask_hbm.own_hbm), channel_id=1, source_target_pairs={{0,64},{8,72},{16,80},{24,88},{32,96},{40,104},{48,112},{56,120},{... | collective-permute-start | bytes 405512 | tf_op jit(solution)/shard_map/ppermute | solution.py:598
  13.7 0.9 copy-done.7
  14.6 0.9 copy-done.9
  15.6 11.0 %attend_prefix.2 = (f32[80,1024]{1,0:T(8,128)S(1)}, f32[8,1024]{1,0:T(8,128)S(1)}) custom-call(bf16[528,128]{1,0:T(8,128)(2,1)S(1)} %copy-done.9, bf16[1024,128]{1,0:T(8,128)(2,1)S(1)} %bitcast.21, bf16[1024,128]{1,0:T(8,128)(2,1)S(1)} %collective-permute-done.7.refs_1_), custom_call_target="tpu_custom_call" | custom-call | flops 2516582400 | bytes 524288 | tf_op jit(solution)/shard_map/attend_prefix/pallas_call | solution.py:286
  26.5 0.0 collective-permute-done.6.ask_hbm
  26.6 0.0 collective-permute-done.5.refs_6_.refs_4_
  26.6 0.0 collective-permute-done.3.refs_2_.refs_0_
  26.6 0.1 collective-permute-start.12
  26.7 0.5 collective-permute-start.13
  27.2 0.1 collective-permute-start.14
  27.3 0.4 collective-permute-start.8
  27.7 0.0 collective-permute-done.w1
  27.8 0.0 copy-start.11
  27.8 4.0 %collective-permute-start.2 = (bf16[2,128,1024]{2,1,0:T(8,128)(2,1)S(1)}, bf16[2,128,1024]{2,1,0:T(8,128)(2,1)S(1)}, u32[]{:S(2)}, u32[]{:S(2)}) collective-permute-start(bf16[2,128,1024]{2,1,0:T(8,128)(2,1)S(1)} %constant_dynamic-update-slice_fusion), channel_id=1, source_target_pairs={{0,2},{1,3},{2,0},{3,1},{4,6},{5,7},{6,4},{7,5},{8,10},{9,11},{10,... | collective-permute-start | bytes 1572872 | tf_op jit(solution)/shard_map/ppermute | solution.py:641
  31.7 0.8 collective-permute-start.11
  32.6 3.5 %collective-permute-start.10 = (bf16[528,128]{1,0:T(8,128)(2,1)S(1)}, bf16[528,128]{1,0:T(8,128)(2,1)S(1)}, u32[]{:S(2)}, u32[]{:S(2)}) collective-permute-start(bf16[528,128]{1,0:T(8,128)(2,1)S(1)} %copy-done.8), channel_id=1, source_target_pairs={{0,48},{8,56},{16,0},{24,8},{32,16},{40,24},{48,32},{56,40},{64,11... | collective-permute-start | bytes 405512 | tf_op jit(solution)/shard_map/ppermute | solution.py:602
  36.1 0.0 collective-permute-done.14.refs_7_.refs_5_
  36.1 42.2 %attend_prefix.3 = (f32[80,1024]{1,0:T(8,128)S(1)}, f32[8,1024]{1,0:T(8,128)S(1)}) custom-call(bf16[528,128]{1,0:T(8,128)(2,1)S(1)} %collective-permute-done.6.ask_hbm, bf16[1024,128]{1,0:T(8,128)(2,1)S(1)} %bitcast.22, bf16[1024,128]{1,0:T(8,128)(2,1)S(1)} %collective-permute-done.7.refs_1_, bf16[1024,128]{1,0:T(8,128)(2,1)S(1)} %collective-permute-done.3.refs_2_.refs_0_, ...), custom_call_target="tpu_custom_call" | custom-call | flops 10066329600 | bytes 2097152 | tf_op jit(solution)/shard_map/attend_prefix/pallas_call | solution.py:286
  78.4 0.1 collective-permute-start.15
  78.5 0.5 collective-permute-start.16
  79.0 0.1 collective-permute-start.17
  79.1 0.7 collective-permute-done.15.refs_3_.refs_9_
  79.8 0.2 collective-permute-done.16.refs_5_.refs_11_
  80.0 0.3 collective-permute-done.17.refs_7_.refs_13_
  80.4 8.1 %attend_partner.1 = (f32[72,1024]{1,0:T(8,128)S(1)}, f32[80,1024]{1,0:T(8,128)S(1)}, f32[8,1024]{1,0:T(8,128)S(1)}) custom-call(bf16[528,128]{1,0:T(8,128)(2,1)S(1)} %collective-permute-done.6.ask_hbm, bf16[528,128]{1,0:T(8,128)(2,1)S(1)} %copy-done.10, f32[8,1024]{1,0:T(8,128)S(1)} %copy-done.11, f32[80,1024]{1,0:T(8,128)S(1)} %get-tuple-element.55.o_in, ...), custom_call_target="tpu_custom_call" | custom-call | flops 1887436800 | bytes 393216 | tf_op jit(solution)/shard_map/attend_partner/pallas_call | solution.py:385
  88.5 0.0 copy-start.1
  88.5 0.0 copy-start.4
  88.5 0.0 copy-start.5
  88.5 0.0 copy-start.6
  88.5 0.3 collective-permute-start.20
  88.8 0.3 collective-permute-start.19
  89.1 0.2 collective-permute-start.21
  89.3 37.0 %attend_own.1 = (f32[80,1024]{1,0:T(8,128)S(1)}, f32[8,1024]{1,0:T(8,128)S(1)}) custom-call(bf16[528,128]{1,0:T(8,128)(2,1)S(1)} %copy-done.10, f32[8,1024]{1,0:T(8,128)S(1)} %copy-done.11, f32[80,1024]{1,0:T(8,128)S(1)} %get-tuple-element.62.o_in, f32[8,1024]{1,0:T(8,128)S(1)} %get-tuple-element.63.m_in, ...), custom_call_target="tpu_custom_call" | custom-call | flops 11324620800 | bytes 2359296 | tf_op jit(solution)/shard_map/attend_own/pallas_call | solution.py:454
  126.3 0.1 join.1
  126.5 9.5 %all_to_all.15.att_ref = bf16[8,64,128]{2,1,0:T(8,128)(2,1)S(1)} all-to-all(bf16[8,64,128]{2,1,0:T(8,128)(2,1)S(1)} %bitcast.13), channel_id=1, replica_groups=mesh['seq'=16,'tp'=8] {'tp'}, dimensions={0} | all-to-all | bytes 262144 | tf_op jit(solution)/shard_map/all_to_all | solution.py:662
  136.0 0.9 mix.1
  136.9 38.2 %all_to_all.16 = bf16[8,64,1152]{2,1,0:T(8,128)(2,1)S(1)} all-to-all(bf16[8,64,1152]{2,1,0:T(8,128)(2,1)S(1)} %get-tuple-element.70), channel_id=1, replica_groups={{0,16,32,48,64,80,96,112},{8,24,40,56,72,88,104,120},{1,17,33,49,65,81,..., dimensions={0} | all-to-all | bytes 2359296 | tf_op jit(solution)/shard_map/all_to_all | solution.py:671
  175.1 7.4 %experts.1 = bf16[512,1024]{1,0:T(8,128)(2,1)S(1)} custom-call(bf16[512,1152]{1,0:T(8,128)(2,1)S(1)} %bitcast.11, bf16[2,1024,1024]{2,1,0:T(8,128)(2,1)S(1)} %copy-done, bf16[2,1024,1024]{2,1,0:T(8,128)(2,1)S(1)} %collective-permute-done.20.wi_peer, bf16[2,512,1024]{2,1,0:T(8,128)(2,1)S(1)} %copy-done.2, ...), custom_call_target="tpu_custom_call" | custom-call | tf_op jit(solution)/shard_map/experts/pallas_call | solution.py:565
  182.6 20.0 %all_to_all.17 = bf16[8,64,1024]{2,1,0:T(8,128)(2,1)S(1)} all-to-all(bf16[8,64,1024]{2,1,0:T(8,128)(2,1)S(1)} %bitcast.12), channel_id=1, replica_groups={{0,16,32,48,64,80,96,112},{8,24,40,56,72,88,104,120},{1,17,33,49,65,81,..., dimensions={0} | all-to-all | bytes 2097152 | tf_op jit(solution)/shard_map/all_to_all | solution.py:675
  202.6 0.2 convert_reduce_fusion
  202.8 0.7 add_convert_fusion
  (35 shorter events, 0.1 us)
Async XLA Ops:
  0.6 10.2 %collective-permute-start.7 = (bf16[1024,128]{1,0:T(8,128)(2,1)}, bf16[1024,128]{1,0:T(8,128)(2,1)S(1)}, u32[]{:S(2)}, u32[]{:S(2)}) collective-permute-start(bf16[1024,128]{1,0:T(8,128)(2,1)} %bitcast.17), channel_id=1, source_target_pairs={{0,8},{8,0},{16,24},{24,16},{32,40},{40,32},{48,56},{56,48},{64,72... | collective-permute-start | bytes 786440 | tf_op jit(solution)/shard_map/ppermute | solution.py:595
  0.7 25.8 %collective-permute-start.5 = (bf16[1024,128]{1,0:T(8,128)(2,1)}, bf16[1024,128]{1,0:T(8,128)(2,1)S(1)}, u32[]{:S(2)}, u32[]{:S(2)}) collective-permute-start(bf16[1024,128]{1,0:T(8,128)(2,1)} %bitcast.18), channel_id=1, source_target_pairs={{0,32},{8,40},{16,48},{24,56},{32,0},{40,8},{48,16},{56,24},{64,96... | collective-permute-start | bytes 786440 | tf_op jit(solution)/shard_map/ppermute | solution.py:602
  4.1 22.5 %collective-permute-start.4 = (bf16[1024,128]{1,0:T(8,128)(2,1)}, bf16[1024,128]{1,0:T(8,128)(2,1)S(1)}, u32[]{:S(2)}, u32[]{:S(2)}) collective-permute-start(bf16[1024,128]{1,0:T(8,128)(2,1)} %bitcast.19), channel_id=1, source_target_pairs={{0,48},{8,56},{16,0},{24,8},{32,16},{40,24},{48,32},{56,40},{64,11... | collective-permute-start | bytes 786440 | tf_op jit(solution)/shard_map/ppermute | solution.py:602
  5.1 21.4 %collective-permute-start.3 = (bf16[1024,128]{1,0:T(8,128)(2,1)}, bf16[1024,128]{1,0:T(8,128)(2,1)S(1)}, u32[]{:S(2)}, u32[]{:S(2)}) collective-permute-start(bf16[1024,128]{1,0:T(8,128)(2,1)} %bitcast.20), channel_id=1, source_target_pairs={{0,16},{8,24},{16,32},{24,40},{32,48},{40,56},{48,0},{56,8},{64,80... | collective-permute-start | bytes 786440 | tf_op jit(solution)/shard_map/ppermute | solution.py:602
  6.1 21.6 %collective-permute-start = (bf16[1,128,1024]{2,1,0:T(8,128)(2,1)}, bf16[1,128,1024]{2,1,0:T(8,128)(2,1)S(1)}, u32[]{:S(2)}, u32[]{:S(2)}) collective-permute-start(bf16[1,128,1024]{2,1,0:T(8,128)(2,1)} %w0.1), channel_id=1, source_target_pairs={{0,4},{1,5},{2,6},{3,7},{4,0},{5,1},{6,2},{7,3},{8,12},{9,13},{10,... | collective-permute-start | bytes 786440 | tf_op jit(solution)/shard_map/ppermute | solution.py:607
  10.9 16.8 %copy-start.3 = (bf16[1,128,1024]{2,1,0:T(8,128)(2,1)S(1)}, bf16[1,128,1024]{2,1,0:T(8,128)(2,1)}, u32[]{:S(2)}) copy-start(bf16[1,128,1024]{2,1,0:T(8,128)(2,1)} %w0.1) | copy-start | bytes 786436
  10.9 15.7 %collective-permute-start.6 = (bf16[528,128]{1,0:T(8,128)(2,1)}, bf16[528,128]{1,0:T(8,128)(2,1)S(1)}, u32[]{:S(2)}, u32[]{:S(2)}) collective-permute-start(bf16[528,128]{1,0:T(8,128)(2,1)} %get-tuple-element.38.ask_hbm.own_hbm), channel_id=1, source_target_pairs={{0,64},{8,72},{16,80},{24,88},{32,96},{40,104},{48,112},{56,120},{... | collective-permute-start | bytes 405512 | tf_op jit(solution)/shard_map/ppermute | solution.py:598
  13.7 0.9 copy-start.7
  14.6 0.9 copy-start.9
  15.6 11.7 %copy-start.8 = (bf16[528,128]{1,0:T(8,128)(2,1)S(1)}, bf16[528,128]{1,0:T(8,128)(2,1)}, u32[]{:S(2)}) copy-start(bf16[528,128]{1,0:T(8,128)(2,1)} %get-tuple-element.45.refs_0_.refs_6_) | copy-start | bytes 405508
  26.6 5.2 %collective-permute-start.12 = (bf16[1024,128]{1,0:T(8,128)(2,1)S(1)}, bf16[1024,128]{1,0:T(8,128)(2,1)S(1)}, u32[]{:S(2)}, u32[]{:S(2)}) collective-permute-start(bf16[1024,128]{1,0:T(8,128)(2,1)S(1)} %collective-permute-done.3.refs_2_.refs_0_), channel_id=1, source_target_pairs={{0,8},{8,0},{16,24},{24,16},{32,40},{40,32},{48,56},{56,48},{64,72... | collective-permute-start | bytes 786440 | tf_op jit(solution)/shard_map/ppermute | solution.py:595
  26.7 5.9 %collective-permute-start.13 = (bf16[1024,128]{1,0:T(8,128)(2,1)S(1)}, bf16[1024,128]{1,0:T(8,128)(2,1)S(1)}, u32[]{:S(2)}, u32[]{:S(2)}) collective-permute-start(bf16[1024,128]{1,0:T(8,128)(2,1)S(1)} %collective-permute-done.4.refs_4_.refs_2_), channel_id=1, source_target_pairs={{0,8},{8,0},{16,24},{24,16},{32,40},{40,32},{48,56},{56,48},{64,72... | collective-permute-start | bytes 786440 | tf_op jit(solution)/shard_map/ppermute | solution.py:595
  27.2 8.9 %collective-permute-start.14 = (bf16[1024,128]{1,0:T(8,128)(2,1)S(1)}, bf16[1024,128]{1,0:T(8,128)(2,1)S(1)}, u32[]{:S(2)}, u32[]{:S(2)}) collective-permute-start(bf16[1024,128]{1,0:T(8,128)(2,1)S(1)} %collective-permute-done.5.refs_6_.refs_4_), channel_id=1, source_target_pairs={{0,8},{8,0},{16,24},{24,16},{32,40},{40,32},{48,56},{56,48},{64,72... | collective-permute-start | bytes 786440 | tf_op jit(solution)/shard_map/ppermute | solution.py:595
  27.3 4.5 %collective-permute-start.8 = (bf16[528,128]{1,0:T(8,128)(2,1)S(1)}, bf16[528,128]{1,0:T(8,128)(2,1)S(1)}, u32[]{:S(2)}, u32[]{:S(2)}) collective-permute-start(bf16[528,128]{1,0:T(8,128)(2,1)S(1)} %copy-done.8), channel_id=1, source_target_pairs={{0,8},{8,0},{16,24},{24,16},{32,40},{40,32},{48,56},{56,48},{64,72... | collective-permute-start | bytes 405512 | tf_op jit(solution)/shard_map/ppermute | solution.py:595
  27.7 52.6 %copy-start.10 = (bf16[528,128]{1,0:T(8,128)(2,1)S(1)}, bf16[528,128]{1,0:T(8,128)(2,1)}, u32[]{:S(2)}) copy-start(bf16[528,128]{1,0:T(8,128)(2,1)} %get-tuple-element.38.ask_hbm.own_hbm) | copy-start | bytes 405508
  27.8 52.6 %copy-start.11 = (f32[8,1024]{1,0:T(8,128)S(1)}, f32[8,1024]{1,0:T(8,128)}, u32[]{:S(2)}) copy-start(f32[8,1024]{1,0:T(8,128)} %get-tuple-element.39.row_ref) | copy-start | bytes 98308
  27.8 60.7 %collective-permute-start.2 = (bf16[2,128,1024]{2,1,0:T(8,128)(2,1)S(1)}, bf16[2,128,1024]{2,1,0:T(8,128)(2,1)S(1)}, u32[]{:S(2)}, u32[]{:S(2)}) collective-permute-start(bf16[2,128,1024]{2,1,0:T(8,128)(2,1)S(1)} %constant_dynamic-update-slice_fusion), channel_id=1, source_target_pairs={{0,2},{1,3},{2,0},{3,1},{4,6},{5,7},{6,4},{7,5},{8,10},{9,11},{10,... | collective-permute-start | bytes 1572872 | tf_op jit(solution)/shard_map/ppermute | solution.py:641
  31.7 56.7 %collective-permute-start.1 = (bf16[2,128,1024]{2,1,0:T(8,128)(2,1)S(1)}, bf16[2,128,1024]{2,1,0:T(8,128)(2,1)S(1)}, u32[]{:S(2)}, u32[]{:S(2)}) collective-permute-start(bf16[2,128,1024]{2,1,0:T(8,128)(2,1)S(1)} %constant_dynamic-update-slice_fusion), channel_id=1, source_target_pairs={{0,1},{1,2},{2,3},{3,0},{4,5},{5,6},{6,7},{7,4},{8,11},{9,8},{10,9... | collective-permute-start | bytes 1572872 | tf_op jit(solution)/shard_map/ppermute | solution.py:640
  31.7 46.6 %collective-permute-start.11 = (bf16[528,128]{1,0:T(8,128)(2,1)S(1)}, bf16[528,128]{1,0:T(8,128)(2,1)S(1)}, u32[]{:S(2)}, u32[]{:S(2)}) collective-permute-start(bf16[528,128]{1,0:T(8,128)(2,1)S(1)} %copy-done.8), channel_id=1, source_target_pairs={{0,32},{8,40},{16,48},{24,56},{32,0},{40,8},{48,16},{56,24},{64,96... | collective-permute-start | bytes 405512 | tf_op jit(solution)/shard_map/ppermute | solution.py:602
  32.6 45.8 %collective-permute-start.10 = (bf16[528,128]{1,0:T(8,128)(2,1)S(1)}, bf16[528,128]{1,0:T(8,128)(2,1)S(1)}, u32[]{:S(2)}, u32[]{:S(2)}) collective-permute-start(bf16[528,128]{1,0:T(8,128)(2,1)S(1)} %copy-done.8), channel_id=1, source_target_pairs={{0,48},{8,56},{16,0},{24,8},{32,16},{40,24},{48,32},{56,40},{64,11... | collective-permute-start | bytes 405512 | tf_op jit(solution)/shard_map/ppermute | solution.py:602
  36.1 42.3 %collective-permute-start.9 = (bf16[528,128]{1,0:T(8,128)(2,1)S(1)}, bf16[528,128]{1,0:T(8,128)(2,1)S(1)}, u32[]{:S(2)}, u32[]{:S(2)}) collective-permute-start(bf16[528,128]{1,0:T(8,128)(2,1)S(1)} %copy-done.8), channel_id=1, source_target_pairs={{0,16},{8,24},{16,32},{24,40},{32,48},{40,56},{48,0},{56,8},{64,80... | collective-permute-start | bytes 405512 | tf_op jit(solution)/shard_map/ppermute | solution.py:602
  78.4 1.4 collective-permute-start.15
  78.5 1.5 collective-permute-start.16
  79.0 1.4 collective-permute-start.17
  80.3 8.1 %copy-start = (bf16[2,1024,1024]{2,1,0:T(8,128)(2,1)S(1)}, bf16[2,1024,1024]{2,1,0:T(8,128)(2,1)}, u32[]{:S(2)}) copy-start(bf16[2,1024,1024]{2,1,0:T(8,128)(2,1)} %wi_own.1) | copy-start | bytes 12582916
  80.3 8.8 %copy-start.2 = (bf16[2,512,1024]{2,1,0:T(8,128)(2,1)S(1)}, bf16[2,512,1024]{2,1,0:T(8,128)(2,1)}, u32[]{:S(2)}) copy-start(bf16[2,512,1024]{2,1,0:T(8,128)(2,1)} %wo_own.1) | copy-start | bytes 6291460
  88.5 47.5 %copy-start.1 = (bf16[512,1024]{1,0:T(8,128)(2,1)S(1)}, bf16[512,1024]{1,0:T(8,128)(2,1)}, u32[]{:S(2)}) copy-start(bf16[512,1024]{1,0:T(8,128)(2,1)} %tok_hbm.3) | copy-start | bytes 3145732
  88.5 47.5 %copy-start.4 = (f32[1024]{0:T(1024)S(1)}, f32[1024]{0:T(1024)}, u32[]{:S(2)}) copy-start(f32[1024]{0:T(1024)} %param.17) | copy-start | bytes 12292
  88.5 47.5 %copy-start.5 = (s32[64,8]{0,1:T(8,128)S(1)}, s32[64,8]{0,1:T(8,128)}, u32[]{:S(2)}) copy-start(s32[64,8]{0,1:T(8,128)} %param.20) | copy-start | bytes 6148
  88.5 47.5 %copy-start.6 = (f32[64,8]{0,1:T(8,128)S(1)}, f32[64,8]{0,1:T(8,128)}, u32[]{:S(2)}) copy-start(f32[64,8]{0,1:T(8,128)} %param.21) | copy-start | bytes 6148
  88.5 86.6 %collective-permute-start.20 = (bf16[2,1024,1024]{2,1,0:T(8,128)(2,1)S(1)}, bf16[2,1024,1024]{2,1,0:T(8,128)(2,1)S(1)}, u32[]{:S(2)}, u32[]{:S(2)}) collective-permute-start(bf16[2,1024,1024]{2,1,0:T(8,128)(2,1)S(1)} %copy-done), channel_id=1, source_target_pairs={{0,8},{8,0},{16,24},{24,16},{32,40},{40,32},{48,56},{56,48},{64,72... | collective-permute-start | bytes 12582920 | tf_op jit(solution)/shard_map/ppermute | solution.py:595
  88.8 37.5 %collective-permute-start.18 = (f32[72,1024]{1,0:T(8,128)S(1)}, f32[72,1024]{1,0:T(8,128)S(1)}, u32[]{:S(2)}, u32[]{:S(2)}) collective-permute-start(f32[72,1024]{1,0:T(8,128)S(1)} %get-tuple-element.66), channel_id=1, source_target_pairs={{0,64},{8,72},{16,80},{24,88},{32,96},{40,104},{48,112},{56,120},{... | collective-permute-start | bytes 884744 | tf_op jit(solution)/shard_map/ppermute | solution.py:598
  88.8 47.2 %collective-permute-start.19 = (bf16[2,128,1024]{2,1,0:T(8,128)(2,1)S(1)}, bf16[2,128,1024]{2,1,0:T(8,128)(2,1)S(1)}, u32[]{:S(2)}, u32[]{:S(2)}) collective-permute-start(bf16[2,128,1024]{2,1,0:T(8,128)(2,1)S(1)} %collective-permute-done.1.w2), channel_id=1, source_target_pairs={{0,8},{8,0},{16,24},{24,16},{32,40},{40,32},{48,56},{56,48},{64,72... | collective-permute-start | bytes 1572872 | tf_op jit(solution)/shard_map/ppermute | solution.py:595
  89.1 86.0 %collective-permute-start.21 = (bf16[2,512,1024]{2,1,0:T(8,128)(2,1)S(1)}, bf16[2,512,1024]{2,1,0:T(8,128)(2,1)S(1)}, u32[]{:S(2)}, u32[]{:S(2)}) collective-permute-start(bf16[2,512,1024]{2,1,0:T(8,128)(2,1)S(1)} %copy-done.2), channel_id=1, source_target_pairs={{0,8},{8,0},{16,24},{24,16},{32,40},{40,32},{48,56},{56,48},{64,72... | collective-permute-start | bytes 6291464 | tf_op jit(solution)/shard_map/ppermute | solution.py:595

commit v3 on v2

--- a/solution.py
+++ b/solution.py
@@ -14,7 +14,7 @@
 TD = 512
 PRE = 1024
 ROWS = 64
-TQ = 512
+TQ = 1024
 NQ = 2 * TD
 SEG_AT = TD
 PAY = SEG_AT + 16
@@ -540,12 +540,12 @@
         number = (x * 8 + y * 2 + (c if e < 2 else 1 - c)) * 2 + e % 2
 
         def half(h, _):
-            rows = pl.ds(pl.multiple_of(h * 256, 256), 256)
+            rows = pl.ds(h * 512, 512)
             joined = jnp.dot(x_ref[rows, :1024], wi[e % 2], preferred_element_type=F32)
             g = joined[:, :512]
             hidden = (g / (1.0 + jnp.exp(-g)) * joined[:, 512:]).astype(BF)
             o = jnp.dot(hidden, wo[e % 2], preferred_element_type=F32).astype(BF).astype(F32)
-            lane = lax.broadcasted_iota(jnp.int32, (256, 128), 1)
+            lane = lax.broadcasted_iota(jnp.int32, (512, 128), 1)
             hit = (lane == number) | (lane == number + 32)
             table = x_ref[rows, 1024:].astype(F32)
             gate = jnp.sum(jnp.where(hit, table, 0.0), axis=1, keepdims=True)
@@ -558,7 +558,7 @@
                 out_ref[rows, :] = o.astype(BF)
             return 0
 
-        lax.fori_loop(0, 2, half, 0, unroll=2)
+        half(0, 0)
 
 
 def expert_call(x, wi_own, wi_peer, wo_own, wo_peer):

time: 203 us -> 194 us (0.956)
  blocking collectives: 67.8 us -> 61.7 us
  Pallas kernels: 110 us -> 107 us
    all_to_all x1, blocking collectives: 38.2 us -> 31.6 us  [body(): lax.all_to_all(copies, 'seq', 0, 0, axis_index_groups=CHIP_GROUPS, tiled=...]
    pallas_call x1, Pallas kernels: 8.09 us -> 5.8 us  [partner_call(): pl.pallas_call(partner_kernel, in_specs=[HBM, HBM] + [VM] * 5 + [HBM] * 8...]
  transfers between devices with their start and end apart: 22 -> 22, of which waited for: 3 -> 3; matrix products, arithmetic and copies ran while one was open for 0% -> 0% of each run, Pallas kernels for 50% -> 51%
where the time goes in v3:
time: 194 us
  Pallas kernels  107 us (55%)
  blocking collectives  61.7 us (32%)
  starting transfers between devices  20.7 us (11%)
  local copies, waits for them, and re-layouts  1.95 us (1%)
    pallas_call x2, Pallas kernels, begin_call(): pl.pallas_call(functools.partial(begin_kernel, count=count), in_specs=[HB...  52.9 us
    pallas_call x1, Pallas kernels, own_call(): pl.pallas_call(own_kernel, in_specs=[HBM, VM, VM, VM] + [HBM] * 14, out_s...  36.5 us
    all_to_all x1, blocking collectives, body(): lax.all_to_all(copies, 'seq', 0, 0, axis_index_groups=CHIP_GROUPS, tiled=...  31.6 us
    all_to_all x1, blocking collectives, body(): lax.all_to_all(partial.reshape(8, ROWS, 1024), 'seq', 0, 0, axis_index_gr...  20.2 us
    ppermute x6, starting transfers between devices, round_y(): lax.ppermute(v, 'seq', seq_perm(lambda a, b, d, k=k: (a, (b + k) % 4, d)))  11.1 us
    all_to_all x1, blocking collectives, body(): lax.all_to_all(attended.reshape(8, ROWS, 128), 'tp', 0, 0, tiled=True)  9.88 us
    pallas_call x1, Pallas kernels, expert_call(): pl.pallas_call(expert_kernel, in_specs=[VM] * 5, out_specs=VM, scratch_sh...  7.12 us
    pallas_call x1, Pallas kernels, partner_call(): pl.pallas_call(partner_kernel, in_specs=[HBM, HBM] + [VM] * 5 + [HBM] * 8...  5.8 us
  transfers between devices with their start and end apart: 22, of which 3 were waited for; matrix products, arithmetic and copies ran while one was open for 0% of the time, Pallas kernels for 51%

profile of v3, /device:TPU:0, one launch (start us, length us, event | category | flops | bytes accessed | tf_op | source)
XLA Modules:
  0.0 194.1 jit_solution(3713121365655107566)
XLA Ops:
  0.6 0.1 collective-permute-start.7
  0.7 3.4 %collective-permute-start.5 = (bf16[1024,128]{1,0:T(8,128)(2,1)}, bf16[1024,128]{1,0:T(8,128)(2,1)S(1)}, u32[]{:S(2)}, u32[]{:S(2)}) collective-permute-start(bf16[1024,128]{1,0:T(8,128)(2,1)} %bitcast.18), channel_id=1, source_target_pairs={{0,32},{8,40},{16,48},{24,56},{32,0},{40,8},{48,16},{56,24},{64,96... | collective-permute-start | bytes 786440 | tf_op jit(solution)/shard_map/ppermute | solution.py:602
  4.1 1.1 collective-permute-start.4
  5.1 1.0 collective-permute-start.3
  6.1 1.5 collective-permute-start
  7.6 3.3 %project.1 = (bf16[528,128]{1,0:T(8,128)(2,1)}, bf16[528,128]{1,0:T(8,128)(2,1)}, f32[8,1024]{1,0:T(8,128)}, bf16[512,128]{1,0:T(8,128)(2,1)}) custom-call(bf16[512,1024]{1,0:T(8,128)(2,1)} %tok_hbm.3, f32[1,1024]{1,0:T(1,128)} %bitcast.24, bf16[1024,256]{1,0:T(8,128)(2,1)} %bitcast.23, s32[4,128]{1,0:T(4,128)} %bitcast.25), custom_call_target="tpu_custom_call" | custom-call | flops 268435456 | bytes 2097152 | tf_op jit(solution)/shard_map/project/pallas_call | solution.py:610
  10.9 0.0 copy-start.3
  10.9 2.8 %collective-permute-start.6 = (bf16[528,128]{1,0:T(8,128)(2,1)}, bf16[528,128]{1,0:T(8,128)(2,1)S(1)}, u32[]{:S(2)}, u32[]{:S(2)}) collective-permute-start(bf16[528,128]{1,0:T(8,128)(2,1)} %get-tuple-element.38.ask_hbm.own_hbm), channel_id=1, source_target_pairs={{0,64},{8,72},{16,80},{24,88},{32,96},{40,104},{48,112},{56,120},{... | collective-permute-start | bytes 405512 | tf_op jit(solution)/shard_map/ppermute | solution.py:598
  13.7 0.9 copy-done.7
  14.6 0.9 copy-done.9
  15.6 10.9 %attend_prefix.2 = (f32[80,1024]{1,0:T(8,128)S(1)}, f32[8,1024]{1,0:T(8,128)S(1)}) custom-call(bf16[528,128]{1,0:T(8,128)(2,1)S(1)} %copy-done.9, bf16[1024,128]{1,0:T(8,128)(2,1)S(1)} %bitcast.21, bf16[1024,128]{1,0:T(8,128)(2,1)S(1)} %collective-permute-done.7.refs_1_), custom_call_target="tpu_custom_call" | custom-call | flops 2516582400 | bytes 524288 | tf_op jit(solution)/shard_map/attend_prefix/pallas_call | solution.py:286
  26.5 0.0 collective-permute-done.5.refs_6_.refs_4_
  26.5 0.0 collective-permute-done.4.refs_4_.refs_2_
  26.5 0.1 collective-permute-start.12
  26.6 0.5 collective-permute-start.13
  27.1 0.1 collective-permute-start.14
  27.2 0.4 collective-permute-start.8
  27.6 0.0 collective-permute-done.w1
  27.7 0.0 copy-start.11
  27.7 2.6 %collective-permute-start.2 = (bf16[2,128,1024]{2,1,0:T(8,128)(2,1)S(1)}, bf16[2,128,1024]{2,1,0:T(8,128)(2,1)S(1)}, u32[]{:S(2)}, u32[]{:S(2)}) collective-permute-start(bf16[2,128,1024]{2,1,0:T(8,128)(2,1)S(1)} %constant_dynamic-update-slice_fusion), channel_id=1, source_target_pairs={{0,2},{1,3},{2,0},{3,1},{4,6},{5,7},{6,4},{7,5},{8,10},{9,11},{10,... | collective-permute-start | bytes 1572872 | tf_op jit(solution)/shard_map/ppermute | solution.py:641
  30.3 0.0 collective-permute-done.8.refs_1_.refs_7_
  30.3 0.0 collective-permute-start.1
  30.3 3.1 %collective-permute-start.11 = (bf16[528,128]{1,0:T(8,128)(2,1)S(1)}, bf16[528,128]{1,0:T(8,128)(2,1)S(1)}, u32[]{:S(2)}, u32[]{:S(2)}) collective-permute-start(bf16[528,128]{1,0:T(8,128)(2,1)S(1)} %copy-done.8), channel_id=1, source_target_pairs={{0,32},{8,40},{16,48},{24,56},{32,0},{40,8},{48,16},{56,24},{64,96... | collective-permute-start | bytes 405512 | tf_op jit(solution)/shard_map/ppermute | solution.py:602
  33.4 2.6 %collective-permute-start.10 = (bf16[528,128]{1,0:T(8,128)(2,1)S(1)}, bf16[528,128]{1,0:T(8,128)(2,1)S(1)}, u32[]{:S(2)}, u32[]{:S(2)}) collective-permute-start(bf16[528,128]{1,0:T(8,128)(2,1)S(1)} %copy-done.8), channel_id=1, source_target_pairs={{0,48},{8,56},{16,0},{24,8},{32,16},{40,24},{48,32},{56,40},{64,11... | collective-permute-start | bytes 405512 | tf_op jit(solution)/shard_map/ppermute | solution.py:602
  36.1 42.0 %attend_prefix.3 = (f32[80,1024]{1,0:T(8,128)S(1)}, f32[8,1024]{1,0:T(8,128)S(1)}) custom-call(bf16[528,128]{1,0:T(8,128)(2,1)S(1)} %collective-permute-done.6.ask_hbm, bf16[1024,128]{1,0:T(8,128)(2,1)S(1)} %bitcast.22, bf16[1024,128]{1,0:T(8,128)(2,1)S(1)} %collective-permute-done.7.refs_1_, bf16[1024,128]{1,0:T(8,128)(2,1)S(1)} %collective-permute-done.3.refs_2_.refs_0_, ...), custom_call_target="tpu_custom_call" | custom-call | flops 10066329600 | bytes 2097152 | tf_op jit(solution)/shard_map/attend_prefix/pallas_call | solution.py:286
  78.1 0.1 collective-permute-start.15
  78.2 0.5 collective-permute-start.16
  78.7 0.1 collective-permute-start.17
  78.8 0.7 collective-permute-done.15.refs_3_.refs_9_
  79.5 0.2 collective-permute-done.16.refs_5_.refs_11_
  79.7 0.3 collective-permute-done.17.refs_7_.refs_13_
  80.1 5.8 %attend_partner.1 = (f32[72,1024]{1,0:T(8,128)S(1)}, f32[80,1024]{1,0:T(8,128)S(1)}, f32[8,1024]{1,0:T(8,128)S(1)}) custom-call(bf16[528,128]{1,0:T(8,128)(2,1)S(1)} %collective-permute-done.6.ask_hbm, bf16[528,128]{1,0:T(8,128)(2,1)S(1)} %copy-done.10, f32[8,1024]{1,0:T(8,128)S(1)} %copy-done.11, f32[80,1024]{1,0:T(8,128)S(1)} %get-tuple-element.55.o_in, ...), custom_call_target="tpu_custom_call" | custom-call | flops 1887436800 | bytes 393216 | tf_op jit(solution)/shard_map/attend_partner/pallas_call | solution.py:385
  85.9 0.0 copy-start.1
  85.9 0.0 copy-start.4
  85.9 0.0 copy-start.5
  85.9 0.0 copy-start.6
  85.9 0.3 collective-permute-start.20
  86.2 0.3 collective-permute-start.19
  86.5 0.2 collective-permute-start.21
  86.7 36.5 %attend_own.1 = (f32[80,1024]{1,0:T(8,128)S(1)}, f32[8,1024]{1,0:T(8,128)S(1)}) custom-call(bf16[528,128]{1,0:T(8,128)(2,1)S(1)} %copy-done.10, f32[8,1024]{1,0:T(8,128)S(1)} %copy-done.11, f32[80,1024]{1,0:T(8,128)S(1)} %get-tuple-element.62.o_in, f32[8,1024]{1,0:T(8,128)S(1)} %get-tuple-element.63.m_in, ...), custom_call_target="tpu_custom_call" | custom-call | flops 11324620800 | bytes 2359296 | tf_op jit(solution)/shard_map/attend_own/pallas_call | solution.py:454
  123.3 0.1 join.1
  123.4 9.9 %all_to_all.15.att_ref = bf16[8,64,128]{2,1,0:T(8,128)(2,1)S(1)} all-to-all(bf16[8,64,128]{2,1,0:T(8,128)(2,1)S(1)} %bitcast.13), channel_id=1, replica_groups=mesh['seq'=16,'tp'=8] {'tp'}, dimensions={0} | all-to-all | bytes 262144 | tf_op jit(solution)/shard_map/all_to_all | solution.py:662
  133.3 0.9 mix.1
  134.2 31.6 %all_to_all.16 = bf16[8,64,1152]{2,1,0:T(8,128)(2,1)S(1)} all-to-all(bf16[8,64,1152]{2,1,0:T(8,128)(2,1)S(1)} %get-tuple-element.70), channel_id=1, replica_groups={{0,16,32,48,64,80,96,112},{8,24,40,56,72,88,104,120},{1,17,33,49,65,81,..., dimensions={0} | all-to-all | bytes 2359296 | tf_op jit(solution)/shard_map/all_to_all | solution.py:671
  165.8 7.1 %experts.1 = bf16[512,1024]{1,0:T(8,128)(2,1)S(1)} custom-call(bf16[512,1152]{1,0:T(8,128)(2,1)S(1)} %bitcast.11, bf16[2,1024,1024]{2,1,0:T(8,128)(2,1)S(1)} %copy-done, bf16[2,1024,1024]{2,1,0:T(8,128)(2,1)S(1)} %collective-permute-done.20.wi_peer, bf16[2,512,1024]{2,1,0:T(8,128)(2,1)S(1)} %copy-done.2, ...), custom_call_target="tpu_custom_call" | custom-call | tf_op jit(solution)/shard_map/experts/pallas_call | solution.py:565
  173.0 20.2 %all_to_all.17 = bf16[8,64,1024]{2,1,0:T(8,128)(2,1)S(1)} all-to-all(bf16[8,64,1024]{2,1,0:T(8,128)(2,1)S(1)} %bitcast.12), channel_id=1, replica_groups={{0,16,32,48,64,80,96,112},{8,24,40,56,72,88,104,120},{1,17,33,49,65,81,..., dimensions={0} | all-to-all | bytes 2097152 | tf_op jit(solution)/shard_map/all_to_all | solution.py:675
  193.2 0.2 convert_reduce_fusion
  193.4 0.7 add_convert_fusion
  (35 shorter events, 0.1 us)
Async XLA Ops:
  0.6 10.2 %collective-permute-start.7 = (bf16[1024,128]{1,0:T(8,128)(2,1)}, bf16[1024,128]{1,0:T(8,128)(2,1)S(1)}, u32[]{:S(2)}, u32[]{:S(2)}) collective-permute-start(bf16[1024,128]{1,0:T(8,128)(2,1)} %bitcast.17), channel_id=1, source_target_pairs={{0,8},{8,0},{16,24},{24,16},{32,40},{40,32},{48,56},{56,48},{64,72... | collective-permute-start | bytes 786440 | tf_op jit(solution)/shard_map/ppermute | solution.py:595
  0.7 25.8 %collective-permute-start.5 = (bf16[1024,128]{1,0:T(8,128)(2,1)}, bf16[1024,128]{1,0:T(8,128)(2,1)S(1)}, u32[]{:S(2)}, u32[]{:S(2)}) collective-permute-start(bf16[1024,128]{1,0:T(8,128)(2,1)} %bitcast.18), channel_id=1, source_target_pairs={{0,32},{8,40},{16,48},{24,56},{32,0},{40,8},{48,16},{56,24},{64,96... | collective-permute-start | bytes 786440 | tf_op jit(solution)/shard_map/ppermute | solution.py:602
  4.1 22.4 %collective-permute-start.4 = (bf16[1024,128]{1,0:T(8,128)(2,1)}, bf16[1024,128]{1,0:T(8,128)(2,1)S(1)}, u32[]{:S(2)}, u32[]{:S(2)}) collective-permute-start(bf16[1024,128]{1,0:T(8,128)(2,1)} %bitcast.19), channel_id=1, source_target_pairs={{0,48},{8,56},{16,0},{24,8},{32,16},{40,24},{48,32},{56,40},{64,11... | collective-permute-start | bytes 786440 | tf_op jit(solution)/shard_map/ppermute | solution.py:602
  5.1 21.4 %collective-permute-start.3 = (bf16[1024,128]{1,0:T(8,128)(2,1)}, bf16[1024,128]{1,0:T(8,128)(2,1)S(1)}, u32[]{:S(2)}, u32[]{:S(2)}) collective-permute-start(bf16[1024,128]{1,0:T(8,128)(2,1)} %bitcast.20), channel_id=1, source_target_pairs={{0,16},{8,24},{16,32},{24,40},{32,48},{40,56},{48,0},{56,8},{64,80... | collective-permute-start | bytes 786440 | tf_op jit(solution)/shard_map/ppermute | solution.py:602
  6.1 21.5 %collective-permute-start = (bf16[1,128,1024]{2,1,0:T(8,128)(2,1)}, bf16[1,128,1024]{2,1,0:T(8,128)(2,1)S(1)}, u32[]{:S(2)}, u32[]{:S(2)}) collective-permute-start(bf16[1,128,1024]{2,1,0:T(8,128)(2,1)} %w0.1), channel_id=1, source_target_pairs={{0,4},{1,5},{2,6},{3,7},{4,0},{5,1},{6,2},{7,3},{8,12},{9,13},{10,... | collective-permute-start | bytes 786440 | tf_op jit(solution)/shard_map/ppermute | solution.py:607
  10.9 16.7 %copy-start.3 = (bf16[1,128,1024]{2,1,0:T(8,128)(2,1)S(1)}, bf16[1,128,1024]{2,1,0:T(8,128)(2,1)}, u32[]{:S(2)}) copy-start(bf16[1,128,1024]{2,1,0:T(8,128)(2,1)} %w0.1) | copy-start | bytes 786436
  10.9 15.6 %collective-permute-start.6 = (bf16[528,128]{1,0:T(8,128)(2,1)}, bf16[528,128]{1,0:T(8,128)(2,1)S(1)}, u32[]{:S(2)}, u32[]{:S(2)}) collective-permute-start(bf16[528,128]{1,0:T(8,128)(2,1)} %get-tuple-element.38.ask_hbm.own_hbm), channel_id=1, source_target_pairs={{0,64},{8,72},{16,80},{24,88},{32,96},{40,104},{48,112},{56,120},{... | collective-permute-start | bytes 405512 | tf_op jit(solution)/shard_map/ppermute | solution.py:598
  13.7 0.9 copy-start.7
  14.6 0.9 copy-start.9
  15.6 11.6 %copy-start.8 = (bf16[528,128]{1,0:T(8,128)(2,1)S(1)}, bf16[528,128]{1,0:T(8,128)(2,1)}, u32[]{:S(2)}) copy-start(bf16[528,128]{1,0:T(8,128)(2,1)} %get-tuple-element.45.refs_0_.refs_6_) | copy-start | bytes 405508
  26.5 3.8 %collective-permute-start.12 = (bf16[1024,128]{1,0:T(8,128)(2,1)S(1)}, bf16[1024,128]{1,0:T(8,128)(2,1)S(1)}, u32[]{:S(2)}, u32[]{:S(2)}) collective-permute-start(bf16[1024,128]{1,0:T(8,128)(2,1)S(1)} %collective-permute-done.3.refs_2_.refs_0_), channel_id=1, source_target_pairs={{0,8},{8,0},{16,24},{24,16},{32,40},{40,32},{48,56},{56,48},{64,72... | collective-permute-start | bytes 786440 | tf_op jit(solution)/shard_map/ppermute | solution.py:595
  26.6 6.8 %collective-permute-start.13 = (bf16[1024,128]{1,0:T(8,128)(2,1)S(1)}, bf16[1024,128]{1,0:T(8,128)(2,1)S(1)}, u32[]{:S(2)}, u32[]{:S(2)}) collective-permute-start(bf16[1024,128]{1,0:T(8,128)(2,1)S(1)} %collective-permute-done.4.refs_4_.refs_2_), channel_id=1, source_target_pairs={{0,8},{8,0},{16,24},{24,16},{32,40},{40,32},{48,56},{56,48},{64,72... | collective-permute-start | bytes 786440 | tf_op jit(solution)/shard_map/ppermute | solution.py:595
  27.1 8.9 %collective-permute-start.14 = (bf16[1024,128]{1,0:T(8,128)(2,1)S(1)}, bf16[1024,128]{1,0:T(8,128)(2,1)S(1)}, u32[]{:S(2)}, u32[]{:S(2)}) collective-permute-start(bf16[1024,128]{1,0:T(8,128)(2,1)S(1)} %collective-permute-done.5.refs_6_.refs_4_), channel_id=1, source_target_pairs={{0,8},{8,0},{16,24},{24,16},{32,40},{40,32},{48,56},{56,48},{64,72... | collective-permute-start | bytes 786440 | tf_op jit(solution)/shard_map/ppermute | solution.py:595
  27.2 3.1 %collective-permute-start.8 = (bf16[528,128]{1,0:T(8,128)(2,1)S(1)}, bf16[528,128]{1,0:T(8,128)(2,1)S(1)}, u32[]{:S(2)}, u32[]{:S(2)}) collective-permute-start(bf16[528,128]{1,0:T(8,128)(2,1)S(1)} %copy-done.8), channel_id=1, source_target_pairs={{0,8},{8,0},{16,24},{24,16},{32,40},{40,32},{48,56},{56,48},{64,72... | collective-permute-start | bytes 405512 | tf_op jit(solution)/shard_map/ppermute | solution.py:595
  27.7 52.4 %copy-start.10 = (bf16[528,128]{1,0:T(8,128)(2,1)S(1)}, bf16[528,128]{1,0:T(8,128)(2,1)}, u32[]{:S(2)}) copy-start(bf16[528,128]{1,0:T(8,128)(2,1)} %get-tuple-element.38.ask_hbm.own_hbm) | copy-start | bytes 405508
  27.7 52.4 %copy-start.11 = (f32[8,1024]{1,0:T(8,128)S(1)}, f32[8,1024]{1,0:T(8,128)}, u32[]{:S(2)}) copy-start(f32[8,1024]{1,0:T(8,128)} %get-tuple-element.39.row_ref) | copy-start | bytes 98308
  27.7 58.2 %collective-permute-start.2 = (bf16[2,128,1024]{2,1,0:T(8,128)(2,1)S(1)}, bf16[2,128,1024]{2,1,0:T(8,128)(2,1)S(1)}, u32[]{:S(2)}, u32[]{:S(2)}) collective-permute-start(bf16[2,128,1024]{2,1,0:T(8,128)(2,1)S(1)} %constant_dynamic-update-slice_fusion), channel_id=1, source_target_pairs={{0,2},{1,3},{2,0},{3,1},{4,6},{5,7},{6,4},{7,5},{8,10},{9,11},{10,... | collective-permute-start | bytes 1572872 | tf_op jit(solution)/shard_map/ppermute | solution.py:641
  30.3 55.6 %collective-permute-start.1 = (bf16[2,128,1024]{2,1,0:T(8,128)(2,1)S(1)}, bf16[2,128,1024]{2,1,0:T(8,128)(2,1)S(1)}, u32[]{:S(2)}, u32[]{:S(2)}) collective-permute-start(bf16[2,128,1024]{2,1,0:T(8,128)(2,1)S(1)} %constant_dynamic-update-slice_fusion), channel_id=1, source_target_pairs={{0,1},{1,2},{2,3},{3,0},{4,5},{5,6},{6,7},{7,4},{8,11},{9,8},{10,9... | collective-permute-start | bytes 1572872 | tf_op jit(solution)/shard_map/ppermute | solution.py:640
  30.3 47.8 %collective-permute-start.11 = (bf16[528,128]{1,0:T(8,128)(2,1)S(1)}, bf16[528,128]{1,0:T(8,128)(2,1)S(1)}, u32[]{:S(2)}, u32[]{:S(2)}) collective-permute-start(bf16[528,128]{1,0:T(8,128)(2,1)S(1)} %copy-done.8), channel_id=1, source_target_pairs={{0,32},{8,40},{16,48},{24,56},{32,0},{40,8},{48,16},{56,24},{64,96... | collective-permute-start | bytes 405512 | tf_op jit(solution)/shard_map/ppermute | solution.py:602
  33.4 44.7 %collective-permute-start.10 = (bf16[528,128]{1,0:T(8,128)(2,1)S(1)}, bf16[528,128]{1,0:T(8,128)(2,1)S(1)}, u32[]{:S(2)}, u32[]{:S(2)}) collective-permute-start(bf16[528,128]{1,0:T(8,128)(2,1)S(1)} %copy-done.8), channel_id=1, source_target_pairs={{0,48},{8,56},{16,0},{24,8},{32,16},{40,24},{48,32},{56,40},{64,11... | collective-permute-start | bytes 405512 | tf_op jit(solution)/shard_map/ppermute | solution.py:602
  36.0 42.0 %collective-permute-start.9 = (bf16[528,128]{1,0:T(8,128)(2,1)S(1)}, bf16[528,128]{1,0:T(8,128)(2,1)S(1)}, u32[]{:S(2)}, u32[]{:S(2)}) collective-permute-start(bf16[528,128]{1,0:T(8,128)(2,1)S(1)} %copy-done.8), channel_id=1, source_target_pairs={{0,16},{8,24},{16,32},{24,40},{32,48},{40,56},{48,0},{56,8},{64,80... | collective-permute-start | bytes 405512 | tf_op jit(solution)/shard_map/ppermute | solution.py:602
  78.1 1.4 collective-permute-start.15
  78.2 1.5 collective-permute-start.16
  78.7 1.4 collective-permute-start.17
  80.0 5.8 %copy-start = (bf16[2,1024,1024]{2,1,0:T(8,128)(2,1)S(1)}, bf16[2,1024,1024]{2,1,0:T(8,128)(2,1)}, u32[]{:S(2)}) copy-start(bf16[2,1024,1024]{2,1,0:T(8,128)(2,1)} %wi_own.1) | copy-start | bytes 12582916
  80.0 6.5 %copy-start.2 = (bf16[2,512,1024]{2,1,0:T(8,128)(2,1)S(1)}, bf16[2,512,1024]{2,1,0:T(8,128)(2,1)}, u32[]{:S(2)}) copy-start(bf16[2,512,1024]{2,1,0:T(8,128)(2,1)} %wo_own.1) | copy-start | bytes 6291460
  85.9 47.4 %copy-start.1 = (bf16[512,1024]{1,0:T(8,128)(2,1)S(1)}, bf16[512,1024]{1,0:T(8,128)(2,1)}, u32[]{:S(2)}) copy-start(bf16[512,1024]{1,0:T(8,128)(2,1)} %tok_hbm.3) | copy-start | bytes 3145732
  85.9 47.4 %copy-start.4 = (f32[1024]{0:T(1024)S(1)}, f32[1024]{0:T(1024)}, u32[]{:S(2)}) copy-start(f32[1024]{0:T(1024)} %param.17) | copy-start | bytes 12292
  85.9 47.4 %copy-start.5 = (s32[64,8]{0,1:T(8,128)S(1)}, s32[64,8]{0,1:T(8,128)}, u32[]{:S(2)}) copy-start(s32[64,8]{0,1:T(8,128)} %param.20) | copy-start | bytes 6148
  85.9 47.4 %copy-start.6 = (f32[64,8]{0,1:T(8,128)S(1)}, f32[64,8]{0,1:T(8,128)}, u32[]{:S(2)}) copy-start(f32[64,8]{0,1:T(8,128)} %param.21) | copy-start | bytes 6148
  85.9 79.9 %collective-permute-start.20 = (bf16[2,1024,1024]{2,1,0:T(8,128)(2,1)S(1)}, bf16[2,1024,1024]{2,1,0:T(8,128)(2,1)S(1)}, u32[]{:S(2)}, u32[]{:S(2)}) collective-permute-start(bf16[2,1024,1024]{2,1,0:T(8,128)(2,1)S(1)} %copy-done), channel_id=1, source_target_pairs={{0,8},{8,0},{16,24},{24,16},{32,40},{40,32},{48,56},{56,48},{64,72... | collective-permute-start | bytes 12582920 | tf_op jit(solution)/shard_map/ppermute | solution.py:595
  86.2 37.1 %collective-permute-start.18 = (f32[72,1024]{1,0:T(8,128)S(1)}, f32[72,1024]{1,0:T(8,128)S(1)}, u32[]{:S(2)}, u32[]{:S(2)}) collective-permute-start(f32[72,1024]{1,0:T(8,128)S(1)} %get-tuple-element.66), channel_id=1, source_target_pairs={{0,64},{8,72},{16,80},{24,88},{32,96},{40,104},{48,112},{56,120},{... | collective-permute-start | bytes 884744 | tf_op jit(solution)/shard_map/ppermute | solution.py:598
  86.2 47.1 %collective-permute-start.19 = (bf16[2,128,1024]{2,1,0:T(8,128)(2,1)S(1)}, bf16[2,128,1024]{2,1,0:T(8,128)(2,1)S(1)}, u32[]{:S(2)}, u32[]{:S(2)}) collective-permute-start(bf16[2,128,1024]{2,1,0:T(8,128)(2,1)S(1)} %collective-permute-done.1.w2), channel_id=1, source_target_pairs={{0,8},{8,0},{16,24},{24,16},{32,40},{40,32},{48,56},{56,48},{64,72... | collective-permute-start | bytes 1572872 | tf_op jit(solution)/shard_map/ppermute | solution.py:595
  86.5 79.3 %collective-permute-start.21 = (bf16[2,512,1024]{2,1,0:T(8,128)(2,1)S(1)}, bf16[2,512,1024]{2,1,0:T(8,128)(2,1)S(1)}, u32[]{:S(2)}, u32[]{:S(2)}) collective-permute-start(bf16[2,512,1024]{2,1,0:T(8,128)(2,1)S(1)} %copy-done.2), channel_id=1, source_target_pairs={{0,8},{8,0},{16,24},{24,16},{32,40},{40,32},{48,56},{56,48},{64,72... | collective-permute-start | bytes 6291464 | tf_op jit(solution)/shard_map/ppermute | solution.py:595

commit v4 on v3

--- a/solution.py
+++ b/solution.py
@@ -160,7 +160,7 @@
         add_block(buf[j], q_ref, o_ref, m_ref, None)
         return 0
 
-    lax.fori_loop(0, count, block, 0, unroll=2)
+    lax.fori_loop(0, count, block, 0, unroll=4 if count == 8 else 2)
 
 
 def again_prefix(count, buf, q_ref, o_ref, m_ref):

time: 194 us -> 196 us (1.010); the launches traced: 194 us -> 199 us
  blocking collectives: 61.7 us -> 65.9 us
    all_to_all x1, blocking collectives: 31.6 us -> 35.8 us  [body(): lax.all_to_all(copies, 'seq', 0, 0, axis_index_groups=CHIP_GROUPS, tiled=...]
  transfers between devices with their start and end apart: 22 -> 22, of which waited for: 3 -> 3; matrix products, arithmetic and copies ran while one was open for 0% -> 0% of each run, Pallas kernels for 51% -> 50%
where the time goes in v4:
time: 196 us; the launch traced here: 199 us
  Pallas kernels  108 us (55%)
  blocking collectives  65.9 us (34%)
  starting transfers between devices  20.7 us (11%)
    pallas_call x2, Pallas kernels, begin_call(): pl.pallas_call(functools.partial(begin_kernel, count=count), in_specs=[HB...  52.7 us
    pallas_call x1, Pallas kernels, own_call(): pl.pallas_call(own_kernel, in_specs=[HBM, VM, VM, VM] + [HBM] * 14, out_s...  36.7 us
    all_to_all x1, blocking collectives, body(): lax.all_to_all(copies, 'seq', 0, 0, axis_index_groups=CHIP_GROUPS, tiled=...  35.8 us
    all_to_all x1, blocking collectives, body(): lax.all_to_all(partial.reshape(8, ROWS, 1024), 'seq', 0, 0, axis_index_gr...  20.3 us
    all_to_all x1, blocking collectives, body(): lax.all_to_all(attended.reshape(8, ROWS, 128), 'tp', 0, 0, tiled=True)  9.87 us
    ppermute x6, starting transfers between devices, round_y(): lax.ppermute(v, 'seq', seq_perm(lambda a, b, d, k=k: (a, (b + k) % 4, d)))  9.78 us
    pallas_call x1, Pallas kernels, expert_call(): pl.pallas_call(expert_kernel, in_specs=[VM] * 5, out_specs=VM, scratch_sh...  7.12 us
    pallas_call x1, Pallas kernels, partner_call(): pl.pallas_call(partner_kernel, in_specs=[HBM, HBM] + [VM] * 5 + [HBM] * 8...  6.94 us
  transfers between devices with their start and end apart: 22, of which 3 were waited for; matrix products, arithmetic and copies ran while one was open for 0% of the time, Pallas kernels for 50%

profile of v4, /device:TPU:0, one launch (start us, length us, event | category | flops | bytes accessed | tf_op | source)
XLA Modules:
  0.0 199.4 jit_solution(10667953256136282551)
XLA Ops:
  0.6 0.1 collective-permute-start.7
  0.7 3.4 %collective-permute-start.5 = (bf16[1024,128]{1,0:T(8,128)(2,1)}, bf16[1024,128]{1,0:T(8,128)(2,1)S(1)}, u32[]{:S(2)}, u32[]{:S(2)}) collective-permute-start(bf16[1024,128]{1,0:T(8,128)(2,1)} %bitcast.18), channel_id=1, source_target_pairs={{0,32},{8,40},{16,48},{24,56},{32,0},{40,8},{48,16},{56,24},{64,96... | collective-permute-start | bytes 786440 | tf_op jit(solution)/shard_map/ppermute | solution.py:602
  4.1 1.1 collective-permute-start.4
  5.1 1.0 collective-permute-start.3
  6.1 1.5 collective-permute-start
  7.6 3.3 %project.1 = (bf16[528,128]{1,0:T(8,128)(2,1)}, bf16[528,128]{1,0:T(8,128)(2,1)}, f32[8,1024]{1,0:T(8,128)}, bf16[512,128]{1,0:T(8,128)(2,1)}) custom-call(bf16[512,1024]{1,0:T(8,128)(2,1)} %tok_hbm.3, f32[1,1024]{1,0:T(1,128)} %bitcast.24, bf16[1024,256]{1,0:T(8,128)(2,1)} %bitcast.23, s32[4,128]{1,0:T(4,128)} %bitcast.25), custom_call_target="tpu_custom_call" | custom-call | flops 268435456 | bytes 2097152 | tf_op jit(solution)/shard_map/project/pallas_call | solution.py:610
  10.9 0.0 copy-start.3
  10.9 2.8 %collective-permute-start.6 = (bf16[528,128]{1,0:T(8,128)(2,1)}, bf16[528,128]{1,0:T(8,128)(2,1)S(1)}, u32[]{:S(2)}, u32[]{:S(2)}) collective-permute-start(bf16[528,128]{1,0:T(8,128)(2,1)} %get-tuple-element.38.ask_hbm.own_hbm), channel_id=1, source_target_pairs={{0,64},{8,72},{16,80},{24,88},{32,96},{40,104},{48,112},{56,120},{... | collective-permute-start | bytes 405512 | tf_op jit(solution)/shard_map/ppermute | solution.py:598
  13.7 0.9 copy-done.7
  14.6 0.9 copy-done.9
  15.6 10.9 %attend_prefix.2 = (f32[80,1024]{1,0:T(8,128)S(1)}, f32[8,1024]{1,0:T(8,128)S(1)}) custom-call(bf16[528,128]{1,0:T(8,128)(2,1)S(1)} %copy-done.9, bf16[1024,128]{1,0:T(8,128)(2,1)S(1)} %bitcast.21, bf16[1024,128]{1,0:T(8,128)(2,1)S(1)} %collective-permute-done.7.refs_1_), custom_call_target="tpu_custom_call" | custom-call | flops 2516582400 | bytes 524288 | tf_op jit(solution)/shard_map/attend_prefix/pallas_call | solution.py:286
  26.5 0.0 collective-permute-done.5.refs_6_.refs_4_
  26.5 0.0 collective-permute-done.4.refs_4_.refs_2_
  26.5 0.1 collective-permute-start.12
  26.6 0.5 collective-permute-start.13
  27.1 0.1 collective-permute-start.14
  27.2 0.4 collective-permute-start.8
  27.6 0.0 collective-permute-done.w1
  27.7 0.0 copy-start.11
  27.7 4.0 %collective-permute-start.2 = (bf16[2,128,1024]{2,1,0:T(8,128)(2,1)S(1)}, bf16[2,128,1024]{2,1,0:T(8,128)(2,1)S(1)}, u32[]{:S(2)}, u32[]{:S(2)}) collective-permute-start(bf16[2,128,1024]{2,1,0:T(8,128)(2,1)S(1)} %constant_dynamic-update-slice_fusion), channel_id=1, source_target_pairs={{0,2},{1,3},{2,0},{3,1},{4,6},{5,7},{6,4},{7,5},{8,10},{9,11},{10,... | collective-permute-start | bytes 1572872 | tf_op jit(solution)/shard_map/ppermute | solution.py:641
  31.7 0.0 collective-permute-done.8.refs_1_.refs_7_
  31.7 1.7 collective-permute-start.11
  33.4 1.7 collective-permute-start.10
  35.1 1.0 collective-permute-start.9
  36.1 41.8 %attend_prefix.3 = (f32[80,1024]{1,0:T(8,128)S(1)}, f32[8,1024]{1,0:T(8,128)S(1)}) custom-call(bf16[528,128]{1,0:T(8,128)(2,1)S(1)} %collective-permute-done.6.ask_hbm, bf16[1024,128]{1,0:T(8,128)(2,1)S(1)} %bitcast.22, bf16[1024,128]{1,0:T(8,128)(2,1)S(1)} %collective-permute-done.7.refs_1_, bf16[1024,128]{1,0:T(8,128)(2,1)S(1)} %collective-permute-done.3.refs_2_.refs_0_, ...), custom_call_target="tpu_custom_call" | custom-call | flops 10066329600 | bytes 2097152 | tf_op jit(solution)/shard_map/attend_prefix/pallas_call | solution.py:286
  77.9 0.1 collective-permute-start.15
  78.0 0.5 collective-permute-start.16
  78.5 0.1 collective-permute-start.17
  78.6 0.8 collective-permute-done.15.refs_3_.refs_9_
  79.3 0.2 collective-permute-done.16.refs_5_.refs_11_
  79.5 0.3 collective-permute-done.17.refs_7_.refs_13_
  79.8 6.9 %attend_partner.1 = (f32[72,1024]{1,0:T(8,128)S(1)}, f32[80,1024]{1,0:T(8,128)S(1)}, f32[8,1024]{1,0:T(8,128)S(1)}) custom-call(bf16[528,128]{1,0:T(8,128)(2,1)S(1)} %collective-permute-done.6.ask_hbm, bf16[528,128]{1,0:T(8,128)(2,1)S(1)} %copy-done.10, f32[8,1024]{1,0:T(8,128)S(1)} %copy-done.11, f32[80,1024]{1,0:T(8,128)S(1)} %get-tuple-element.55.o_in, ...), custom_call_target="tpu_custom_call" | custom-call | flops 1887436800 | bytes 393216 | tf_op jit(solution)/shard_map/attend_partner/pallas_call | solution.py:385
  86.8 0.0 copy-start.1
  86.8 0.0 copy-start.4
  86.8 0.0 copy-start.5
  86.9 0.0 copy-start.6
  86.9 0.3 collective-permute-start.20
  87.2 0.3 collective-permute-start.19
  87.5 0.2 collective-permute-start.21
  87.7 36.7 %attend_own.1 = (f32[80,1024]{1,0:T(8,128)S(1)}, f32[8,1024]{1,0:T(8,128)S(1)}) custom-call(bf16[528,128]{1,0:T(8,128)(2,1)S(1)} %copy-done.10, f32[8,1024]{1,0:T(8,128)S(1)} %copy-done.11, f32[80,1024]{1,0:T(8,128)S(1)} %get-tuple-element.62.o_in, f32[8,1024]{1,0:T(8,128)S(1)} %get-tuple-element.63.m_in, ...), custom_call_target="tpu_custom_call" | custom-call | flops 11324620800 | bytes 2359296 | tf_op jit(solution)/shard_map/attend_own/pallas_call | solution.py:454
  124.4 0.1 join.1
  124.6 9.9 %all_to_all.15.att_ref = bf16[8,64,128]{2,1,0:T(8,128)(2,1)S(1)} all-to-all(bf16[8,64,128]{2,1,0:T(8,128)(2,1)S(1)} %bitcast.13), channel_id=1, replica_groups=mesh['seq'=16,'tp'=8] {'tp'}, dimensions={0} | all-to-all | bytes 262144 | tf_op jit(solution)/shard_map/all_to_all | solution.py:662
  134.5 0.9 mix.1
  135.4 35.8 %all_to_all.16 = bf16[8,64,1152]{2,1,0:T(8,128)(2,1)S(1)} all-to-all(bf16[8,64,1152]{2,1,0:T(8,128)(2,1)S(1)} %get-tuple-element.70), channel_id=1, replica_groups={{0,16,32,48,64,80,96,112},{8,24,40,56,72,88,104,120},{1,17,33,49,65,81,..., dimensions={0} | all-to-all | bytes 2359296 | tf_op jit(solution)/shard_map/all_to_all | solution.py:671
  171.1 7.1 %experts.1 = bf16[512,1024]{1,0:T(8,128)(2,1)S(1)} custom-call(bf16[512,1152]{1,0:T(8,128)(2,1)S(1)} %bitcast.11, bf16[2,1024,1024]{2,1,0:T(8,128)(2,1)S(1)} %copy-done, bf16[2,1024,1024]{2,1,0:T(8,128)(2,1)S(1)} %collective-permute-done.20.wi_peer, bf16[2,512,1024]{2,1,0:T(8,128)(2,1)S(1)} %copy-done.2, ...), custom_call_target="tpu_custom_call" | custom-call | tf_op jit(solution)/shard_map/experts/pallas_call | solution.py:565
  178.3 20.3 %all_to_all.17 = bf16[8,64,1024]{2,1,0:T(8,128)(2,1)S(1)} all-to-all(bf16[8,64,1024]{2,1,0:T(8,128)(2,1)S(1)} %bitcast.12), channel_id=1, replica_groups={{0,16,32,48,64,80,96,112},{8,24,40,56,72,88,104,120},{1,17,33,49,65,81,..., dimensions={0} | all-to-all | bytes 2097152 | tf_op jit(solution)/shard_map/all_to_all | solution.py:675
  198.5 0.2 convert_reduce_fusion
  198.7 0.7 add_convert_fusion
  (35 shorter events, 0.1 us)
Async XLA Ops:
  0.6 10.2 %collective-permute-start.7 = (bf16[1024,128]{1,0:T(8,128)(2,1)}, bf16[1024,128]{1,0:T(8,128)(2,1)S(1)}, u32[]{:S(2)}, u32[]{:S(2)}) collective-permute-start(bf16[1024,128]{1,0:T(8,128)(2,1)} %bitcast.17), channel_id=1, source_target_pairs={{0,8},{8,0},{16,24},{24,16},{32,40},{40,32},{48,56},{56,48},{64,72... | collective-permute-start | bytes 786440 | tf_op jit(solution)/shard_map/ppermute | solution.py:595
  0.7 25.8 %collective-permute-start.5 = (bf16[1024,128]{1,0:T(8,128)(2,1)}, bf16[1024,128]{1,0:T(8,128)(2,1)S(1)}, u32[]{:S(2)}, u32[]{:S(2)}) collective-permute-start(bf16[1024,128]{1,0:T(8,128)(2,1)} %bitcast.18), channel_id=1, source_target_pairs={{0,32},{8,40},{16,48},{24,56},{32,0},{40,8},{48,16},{56,24},{64,96... | collective-permute-start | bytes 786440 | tf_op jit(solution)/shard_map/ppermute | solution.py:602
  4.1 22.4 %collective-permute-start.4 = (bf16[1024,128]{1,0:T(8,128)(2,1)}, bf16[1024,128]{1,0:T(8,128)(2,1)S(1)}, u32[]{:S(2)}, u32[]{:S(2)}) collective-permute-start(bf16[1024,128]{1,0:T(8,128)(2,1)} %bitcast.19), channel_id=1, source_target_pairs={{0,48},{8,56},{16,0},{24,8},{32,16},{40,24},{48,32},{56,40},{64,11... | collective-permute-start | bytes 786440 | tf_op jit(solution)/shard_map/ppermute | solution.py:602
  5.1 21.4 %collective-permute-start.3 = (bf16[1024,128]{1,0:T(8,128)(2,1)}, bf16[1024,128]{1,0:T(8,128)(2,1)S(1)}, u32[]{:S(2)}, u32[]{:S(2)}) collective-permute-start(bf16[1024,128]{1,0:T(8,128)(2,1)} %bitcast.20), channel_id=1, source_target_pairs={{0,16},{8,24},{16,32},{24,40},{32,48},{40,56},{48,0},{56,8},{64,80... | collective-permute-start | bytes 786440 | tf_op jit(solution)/shard_map/ppermute | solution.py:602
  6.1 21.5 %collective-permute-start = (bf16[1,128,1024]{2,1,0:T(8,128)(2,1)}, bf16[1,128,1024]{2,1,0:T(8,128)(2,1)S(1)}, u32[]{:S(2)}, u32[]{:S(2)}) collective-permute-start(bf16[1,128,1024]{2,1,0:T(8,128)(2,1)} %w0.1), channel_id=1, source_target_pairs={{0,4},{1,5},{2,6},{3,7},{4,0},{5,1},{6,2},{7,3},{8,12},{9,13},{10,... | collective-permute-start | bytes 786440 | tf_op jit(solution)/shard_map/ppermute | solution.py:607
  10.9 16.7 %copy-start.3 = (bf16[1,128,1024]{2,1,0:T(8,128)(2,1)S(1)}, bf16[1,128,1024]{2,1,0:T(8,128)(2,1)}, u32[]{:S(2)}) copy-start(bf16[1,128,1024]{2,1,0:T(8,128)(2,1)} %w0.1) | copy-start | bytes 786436
  10.9 15.6 %collective-permute-start.6 = (bf16[528,128]{1,0:T(8,128)(2,1)}, bf16[528,128]{1,0:T(8,128)(2,1)S(1)}, u32[]{:S(2)}, u32[]{:S(2)}) collective-permute-start(bf16[528,128]{1,0:T(8,128)(2,1)} %get-tuple-element.38.ask_hbm.own_hbm), channel_id=1, source_target_pairs={{0,64},{8,72},{16,80},{24,88},{32,96},{40,104},{48,112},{56,120},{... | collective-permute-start | bytes 405512 | tf_op jit(solution)/shard_map/ppermute | solution.py:598
  13.7 0.9 copy-start.7
  14.6 0.9 copy-start.9
  15.6 11.6 %copy-start.8 = (bf16[528,128]{1,0:T(8,128)(2,1)S(1)}, bf16[528,128]{1,0:T(8,128)(2,1)}, u32[]{:S(2)}) copy-start(bf16[528,128]{1,0:T(8,128)(2,1)} %get-tuple-element.45.refs_0_.refs_6_) | copy-start | bytes 405508
  26.5 5.2 %collective-permute-start.12 = (bf16[1024,128]{1,0:T(8,128)(2,1)S(1)}, bf16[1024,128]{1,0:T(8,128)(2,1)S(1)}, u32[]{:S(2)}, u32[]{:S(2)}) collective-permute-start(bf16[1024,128]{1,0:T(8,128)(2,1)S(1)} %collective-permute-done.3.refs_2_.refs_0_), channel_id=1, source_target_pairs={{0,8},{8,0},{16,24},{24,16},{32,40},{40,32},{48,56},{56,48},{64,72... | collective-permute-start | bytes 786440 | tf_op jit(solution)/shard_map/ppermute | solution.py:595
  26.6 6.8 %collective-permute-start.13 = (bf16[1024,128]{1,0:T(8,128)(2,1)S(1)}, bf16[1024,128]{1,0:T(8,128)(2,1)S(1)}, u32[]{:S(2)}, u32[]{:S(2)}) collective-permute-start(bf16[1024,128]{1,0:T(8,128)(2,1)S(1)} %collective-permute-done.4.refs_4_.refs_2_), channel_id=1, source_target_pairs={{0,8},{8,0},{16,24},{24,16},{32,40},{40,32},{48,56},{56,48},{64,72... | collective-permute-start | bytes 786440 | tf_op jit(solution)/shard_map/ppermute | solution.py:595
  27.1 8.0 %collective-permute-start.14 = (bf16[1024,128]{1,0:T(8,128)(2,1)S(1)}, bf16[1024,128]{1,0:T(8,128)(2,1)S(1)}, u32[]{:S(2)}, u32[]{:S(2)}) collective-permute-start(bf16[1024,128]{1,0:T(8,128)(2,1)S(1)} %collective-permute-done.5.refs_6_.refs_4_), channel_id=1, source_target_pairs={{0,8},{8,0},{16,24},{24,16},{32,40},{40,32},{48,56},{56,48},{64,72... | collective-permute-start | bytes 786440 | tf_op jit(solution)/shard_map/ppermute | solution.py:595
  27.2 4.5 %collective-permute-start.8 = (bf16[528,128]{1,0:T(8,128)(2,1)S(1)}, bf16[528,128]{1,0:T(8,128)(2,1)S(1)}, u32[]{:S(2)}, u32[]{:S(2)}) collective-permute-start(bf16[528,128]{1,0:T(8,128)(2,1)S(1)} %copy-done.8), channel_id=1, source_target_pairs={{0,8},{8,0},{16,24},{24,16},{32,40},{40,32},{48,56},{56,48},{64,72... | collective-permute-start | bytes 405512 | tf_op jit(solution)/shard_map/ppermute | solution.py:595
  27.7 52.2 %copy-start.10 = (bf16[528,128]{1,0:T(8,128)(2,1)S(1)}, bf16[528,128]{1,0:T(8,128)(2,1)}, u32[]{:S(2)}) copy-start(bf16[528,128]{1,0:T(8,128)(2,1)} %get-tuple-element.38.ask_hbm.own_hbm) | copy-start | bytes 405508
  27.7 52.1 %copy-start.11 = (f32[8,1024]{1,0:T(8,128)S(1)}, f32[8,1024]{1,0:T(8,128)}, u32[]{:S(2)}) copy-start(f32[8,1024]{1,0:T(8,128)} %get-tuple-element.39.row_ref) | copy-start | bytes 98308
  27.7 59.1 %collective-permute-start.2 = (bf16[2,128,1024]{2,1,0:T(8,128)(2,1)S(1)}, bf16[2,128,1024]{2,1,0:T(8,128)(2,1)S(1)}, u32[]{:S(2)}, u32[]{:S(2)}) collective-permute-start(bf16[2,128,1024]{2,1,0:T(8,128)(2,1)S(1)} %constant_dynamic-update-slice_fusion), channel_id=1, source_target_pairs={{0,2},{1,3},{2,0},{3,1},{4,6},{5,7},{6,4},{7,5},{8,10},{9,11},{10,... | collective-permute-start | bytes 1572872 | tf_op jit(solution)/shard_map/ppermute | solution.py:641
  31.7 55.1 %collective-permute-start.1 = (bf16[2,128,1024]{2,1,0:T(8,128)(2,1)S(1)}, bf16[2,128,1024]{2,1,0:T(8,128)(2,1)S(1)}, u32[]{:S(2)}, u32[]{:S(2)}) collective-permute-start(bf16[2,128,1024]{2,1,0:T(8,128)(2,1)S(1)} %constant_dynamic-update-slice_fusion), channel_id=1, source_target_pairs={{0,1},{1,2},{2,3},{3,0},{4,5},{5,6},{6,7},{7,4},{8,11},{9,8},{10,9... | collective-permute-start | bytes 1572872 | tf_op jit(solution)/shard_map/ppermute | solution.py:640
  31.7 46.2 %collective-permute-start.11 = (bf16[528,128]{1,0:T(8,128)(2,1)S(1)}, bf16[528,128]{1,0:T(8,128)(2,1)S(1)}, u32[]{:S(2)}, u32[]{:S(2)}) collective-permute-start(bf16[528,128]{1,0:T(8,128)(2,1)S(1)} %copy-done.8), channel_id=1, source_target_pairs={{0,32},{8,40},{16,48},{24,56},{32,0},{40,8},{48,16},{56,24},{64,96... | collective-permute-start | bytes 405512 | tf_op jit(solution)/shard_map/ppermute | solution.py:602
  33.4 44.4 %collective-permute-start.10 = (bf16[528,128]{1,0:T(8,128)(2,1)S(1)}, bf16[528,128]{1,0:T(8,128)(2,1)S(1)}, u32[]{:S(2)}, u32[]{:S(2)}) collective-permute-start(bf16[528,128]{1,0:T(8,128)(2,1)S(1)} %copy-done.8), channel_id=1, source_target_pairs={{0,48},{8,56},{16,0},{24,8},{32,16},{40,24},{48,32},{56,40},{64,11... | collective-permute-start | bytes 405512 | tf_op jit(solution)/shard_map/ppermute | solution.py:602
  35.1 42.8 %collective-permute-start.9 = (bf16[528,128]{1,0:T(8,128)(2,1)S(1)}, bf16[528,128]{1,0:T(8,128)(2,1)S(1)}, u32[]{:S(2)}, u32[]{:S(2)}) collective-permute-start(bf16[528,128]{1,0:T(8,128)(2,1)S(1)} %copy-done.8), channel_id=1, source_target_pairs={{0,16},{8,24},{16,32},{24,40},{32,48},{40,56},{48,0},{56,8},{64,80... | collective-permute-start | bytes 405512 | tf_op jit(solution)/shard_map/ppermute | solution.py:602
  77.9 1.4 collective-permute-start.15
  78.0 1.5 collective-permute-start.16
  78.5 1.4 collective-permute-start.17
  79.8 7.0 %copy-start = (bf16[2,1024,1024]{2,1,0:T(8,128)(2,1)S(1)}, bf16[2,1024,1024]{2,1,0:T(8,128)(2,1)}, u32[]{:S(2)}) copy-start(bf16[2,1024,1024]{2,1,0:T(8,128)(2,1)} %wi_own.1) | copy-start | bytes 12582916
  79.8 7.6 %copy-start.2 = (bf16[2,512,1024]{2,1,0:T(8,128)(2,1)S(1)}, bf16[2,512,1024]{2,1,0:T(8,128)(2,1)}, u32[]{:S(2)}) copy-start(bf16[2,512,1024]{2,1,0:T(8,128)(2,1)} %wo_own.1) | copy-start | bytes 6291460
  86.8 47.6 %copy-start.1 = (bf16[512,1024]{1,0:T(8,128)(2,1)S(1)}, bf16[512,1024]{1,0:T(8,128)(2,1)}, u32[]{:S(2)}) copy-start(bf16[512,1024]{1,0:T(8,128)(2,1)} %tok_hbm.3) | copy-start | bytes 3145732
  86.8 47.6 %copy-start.4 = (f32[1024]{0:T(1024)S(1)}, f32[1024]{0:T(1024)}, u32[]{:S(2)}) copy-start(f32[1024]{0:T(1024)} %param.17) | copy-start | bytes 12292
  86.8 47.6 %copy-start.5 = (s32[64,8]{0,1:T(8,128)S(1)}, s32[64,8]{0,1:T(8,128)}, u32[]{:S(2)}) copy-start(s32[64,8]{0,1:T(8,128)} %param.20) | copy-start | bytes 6148
  86.9 47.6 %copy-start.6 = (f32[64,8]{0,1:T(8,128)S(1)}, f32[64,8]{0,1:T(8,128)}, u32[]{:S(2)}) copy-start(f32[64,8]{0,1:T(8,128)} %param.21) | copy-start | bytes 6148
  86.9 84.3 %collective-permute-start.20 = (bf16[2,1024,1024]{2,1,0:T(8,128)(2,1)S(1)}, bf16[2,1024,1024]{2,1,0:T(8,128)(2,1)S(1)}, u32[]{:S(2)}, u32[]{:S(2)}) collective-permute-start(bf16[2,1024,1024]{2,1,0:T(8,128)(2,1)S(1)} %copy-done), channel_id=1, source_target_pairs={{0,8},{8,0},{16,24},{24,16},{32,40},{40,32},{48,56},{56,48},{64,72... | collective-permute-start | bytes 12582920 | tf_op jit(solution)/shard_map/ppermute | solution.py:595
  87.2 37.3 %collective-permute-start.18 = (f32[72,1024]{1,0:T(8,128)S(1)}, f32[72,1024]{1,0:T(8,128)S(1)}, u32[]{:S(2)}, u32[]{:S(2)}) collective-permute-start(f32[72,1024]{1,0:T(8,128)S(1)} %get-tuple-element.66), channel_id=1, source_target_pairs={{0,64},{8,72},{16,80},{24,88},{32,96},{40,104},{48,112},{56,120},{... | collective-permute-start | bytes 884744 | tf_op jit(solution)/shard_map/ppermute | solution.py:598
  87.2 47.3 %collective-permute-start.19 = (bf16[2,128,1024]{2,1,0:T(8,128)(2,1)S(1)}, bf16[2,128,1024]{2,1,0:T(8,128)(2,1)S(1)}, u32[]{:S(2)}, u32[]{:S(2)}) collective-permute-start(bf16[2,128,1024]{2,1,0:T(8,128)(2,1)S(1)} %collective-permute-done.1.w2), channel_id=1, source_target_pairs={{0,8},{8,0},{16,24},{24,16},{32,40},{40,32},{48,56},{56,48},{64,72... | collective-permute-start | bytes 1572872 | tf_op jit(solution)/shard_map/ppermute | solution.py:595
  87.5 83.7 %collective-permute-start.21 = (bf16[2,512,1024]{2,1,0:T(8,128)(2,1)S(1)}, bf16[2,512,1024]{2,1,0:T(8,128)(2,1)S(1)}, u32[]{:S(2)}, u32[]{:S(2)}) collective-permute-start(bf16[2,512,1024]{2,1,0:T(8,128)(2,1)S(1)} %copy-done.2), channel_id=1, source_target_pairs={{0,8},{8,0},{16,24},{24,16},{32,40},{40,32},{48,56},{56,48},{64,72... | collective-permute-start | bytes 6291464 | tf_op jit(solution)/shard_map/ppermute | solution.py:595
